TPU v7x, 256 devices: a whole 4x4x8 slice. The times are simulated.
256 devices in a mesh: fluid: 32 (over y, x, core), wall: 8 (over z).
Axes of the slice: x: 4, y: 4, z: 8, core: 2. Of those that a mesh axis runs over, the one named last changes fastest.
Arguments:
- flow_state: float32 [4, 512, 32, 1024], P(None, 'fluid', None, 'wall'), may hold values from -6 to 6
- regions: int32 [512, 32, 1024], P('fluid', None, 'wall'), may hold values from 0 to 127
- obs_tiles: bfloat16 [32, 8, 32, 128, 128], P('fluid', 'wall'), may hold values from -0.5 to 0.5
- measured: bfloat16 [32, 8, 32, 3, 128], P('fluid', 'wall'), may hold values from -6 to 6
- tile_dest: int32 [32, 8, 32], P('fluid', 'wall'), may hold values from 0 to 31, as said below
- cell_list: int32 [32, 8, 32, 4], P('fluid', 'wall'), may hold values from 0 to 511
Outputs:
- velocity_next: float32 [3, 512, 32, 1024], P(None, 'fluid', None, 'wall')
- adjoint: float32 [3, 512, 32, 1024], P(None, 'fluid', None, 'wall')
- sensitivity: float32 [4096], P(('fluid', 'wall'))
Inputs may be any that keep to these rules, and one draw needn't show every extreme that they name: `tile_dest`: each device's list names every fluid block at most 4 times. In each wall column one fluid block is named exactly 4 times by the list of every device of that column.
All inputs are finite; a program needn't handle non-finite values.
Results may differ from a plain program's by a relative error of at most 0.0032.
Values may be sent and summed in bfloat16 or wider, within the bound.
A program may use at most 128 MiB of HBM per device.

v0:
```python
import jax
import jax.numpy as jnp
from jax import lax
from jax.sharding import PartitionSpec as P

REG_DEV = 16


time_step = 0.12
nu_floor = 0.1
nu_spread = 0.9
relax_sq = 4.0
sens_scale = 0.03


def with_halo(block, sides, width):
    for axis, dim in sides:
        count = lax.axis_size(axis)
        forward = [(i, i + 1) for i in range(count - 1)]
        backward = [(target, source) for source, target in forward]
        low = lax.ppermute(
            lax.slice_in_dim(block, block.shape[dim] - width, None, axis=dim), axis, forward
        )
        high = lax.ppermute(lax.slice_in_dim(block, 0, width, axis=dim), axis, backward)
        block = jnp.concatenate([low, block, high], axis=dim)
    return block


def face_differences(padded, spatial):
    extent = padded.shape[spatial]
    upper_cells = lax.slice_in_dim(padded, 1, extent, axis=spatial)
    lower_cells = lax.slice_in_dim(padded, 0, extent - 1, axis=spatial)
    face_jump = upper_cells - lower_cells
    for across in (1, 2, 3):
        if across != spatial:
            face_jump = lax.slice_in_dim(face_jump, 1, face_jump.shape[across] - 1, axis=across)
    return face_jump


def viscosity(face_jump):
    shear_sq = jnp.sum(face_jump * face_jump, axis=0)
    return nu_floor + nu_spread * jnp.power(1.0 + relax_sq * shear_sq, -0.25)


def divergence(face_nus, face_jumps):
    summed = 0.0
    for spatial, nu_face, face_jump in zip((1, 2, 3), face_nus, face_jumps):
        face_flux = nu_face[None] * face_jump
        extent = face_flux.shape[spatial]
        summed = (
            summed
            + lax.slice_in_dim(face_flux, 1, extent, axis=spatial)
            - lax.slice_in_dim(face_flux, 0, extent - 1, axis=spatial)
        )
    return summed


def forward(padded):
    velocity = padded[:3]
    pressure = padded[3:4]
    face_jumps = [face_differences(velocity, spatial) for spatial in (1, 2, 3)]
    face_nus = [viscosity(face_jump) for face_jump in face_jumps]
    halves = []
    for spatial in (1, 2, 3):
        pressure_jump = face_differences(pressure, spatial)
        extent = pressure_jump.shape[spatial]
        halves.append(
            0.5
            * (
                lax.slice_in_dim(pressure_jump, 1, extent, axis=spatial)
                + lax.slice_in_dim(pressure_jump, 0, extent - 1, axis=spatial)
            )
        )
    gradient = jnp.concatenate(halves, axis=0)
    interior = padded[:3, 1:-1, 1:-1, 1:-1]
    velocity_next = interior + time_step * (divergence(face_nus, face_jumps) - gradient)
    return (velocity_next, face_nus)


def adjoint_step(padded_forcing, face_nus):
    face_jumps = [face_differences(padded_forcing, spatial) for spatial in (1, 2, 3)]
    return padded_forcing[:, 1:-1, 1:-1, 1:-1] + time_step * divergence(face_nus, face_jumps)


def body(flow_state, regions, obs_tiles, measured, tile_dest, cell_list):
    rimmed = with_halo(flow_state, (("fluid", 1), ("wall", 3)), 1)
    padded = jnp.pad(rimmed, ((0, 0), (0, 0), (1, 1), (0, 0)))
    velocity_next, face_nus = forward(padded)
    obs_velocity = velocity_next.astype(jnp.bfloat16)
    block_groups = lax.axis_size("fluid")
    width_x = flow_state.shape[1]
    width_y = flow_state.shape[2]
    depth_width = flow_state.shape[3]
    slot_limit = cell_list.shape[3]
    count_tiles = obs_tiles.shape[2]
    total_slots = block_groups * slot_limit
    obs_cells = obs_velocity.reshape(3, width_x * width_y, depth_width)
    target = tile_dest[0, 0]
    same_target = target[:, None] == target[None, :]
    before = jnp.arange(count_tiles)[None, :] < jnp.arange(count_tiles)[:, None]
    slot_rank = jnp.sum((same_target & before).astype(jnp.int32), axis=1)
    index_of_slot = target * slot_limit + slot_rank
    cell_ids = cell_list[0, 0].reshape(total_slots)
    tile_rows = obs_tiles[0, 0]
    measurement_rows = measured[0, 0]
    send_tiles = (
        jnp.zeros((total_slots, depth_width, depth_width), jnp.bfloat16)
        .at[index_of_slot]
        .set(tile_rows)
    )
    outgoing_measurements = (
        jnp.zeros((total_slots, 3, depth_width), jnp.bfloat16)
        .at[index_of_slot]
        .set(measurement_rows)
    )
    received_tiles, received_measurements = (
        lax.all_to_all(
            send_tiles.reshape(block_groups, slot_limit, depth_width, depth_width),
            "fluid",
            split_axis=0,
            concat_axis=0,
            tiled=True,
        ),
        lax.all_to_all(
            outgoing_measurements.reshape(block_groups, slot_limit, 3, depth_width),
            "fluid",
            split_axis=0,
            concat_axis=0,
            tiled=True,
        ),
    )
    received_tiles = received_tiles.reshape(total_slots, depth_width, depth_width)
    received_measurements = received_measurements.reshape(total_slots, 3, depth_width)
    cell_values = jnp.take(obs_cells, cell_ids, axis=1)
    model_velocity = jnp.einsum(
        "mij,cmj->mci", received_tiles, cell_values, preferred_element_type=jnp.float32
    )
    data_residual = (model_velocity - received_measurements.astype(jnp.float32)).astype(
        jnp.bfloat16
    )
    contrib = jnp.einsum(
        "mij,mci->mcj", received_tiles, data_residual, preferred_element_type=jnp.float32
    )
    forcing = (
        jnp.zeros((3, width_x * width_y, depth_width), jnp.float32)
        .at[:, cell_ids]
        .add(jnp.transpose(contrib, (1, 0, 2)))
    )
    forcing = forcing.reshape(3, width_x, width_y, depth_width)
    rim_force = with_halo(forcing, (("fluid", 1), ("wall", 3)), 1)
    padded_forcing = jnp.pad(rim_force, ((0, 0), (0, 0), (1, 1), (0, 0)))
    adjoint = adjoint_step(padded_forcing, face_nus)
    product = jnp.sum(adjoint * velocity_next, axis=0)
    reg_count = REG_DEV * lax.axis_size("wall")
    labels = jnp.arange(reg_count, dtype=jnp.int32)

    def add_slab(running, slab_pair):
        values, slab_ids = slab_pair
        onehot = (slab_ids[:, None] == labels[None, :]).astype(jnp.float32)
        return (running + jnp.dot(values, onehot, precision=lax.Precision.HIGHEST), None)

    partial_sums, _ = lax.scan(
        add_slab,
        jnp.zeros((reg_count,), jnp.float32),
        (product.reshape(width_x, -1), regions.reshape(width_x, -1)),
    )
    owned = lax.psum_scatter(partial_sums, "wall", scatter_dimension=0, tiled=True)
    return (velocity_next, adjoint, sens_scale * owned)


def solution(mesh):
    in_specs = (
        P(None, "fluid", None, "wall"),
        P("fluid", None, "wall"),
        P("fluid", "wall", None, None, None),
        P("fluid", "wall", None, None, None),
        P("fluid", "wall", None),
        P("fluid", "wall", None, None),
    )
    out_specs = (
        P(None, "fluid", None, "wall"),
        P(None, "fluid", None, "wall"),
        P(("fluid", "wall")),
    )
    return jax.shard_map(body, mesh=mesh, in_specs=in_specs, out_specs=out_specs, check_vma=False)
```

profile of v0, /device:TPU:8, one launch (start us, length us, event | category | flops | bytes accessed | tf_op | source)
XLA Modules:
  0.0 210.0 jit_solution(5108690657403877988)
XLA Ops:
  3.4 5.8 %collective-permute-start.1 = (f32[4,1,32,128]{3,2,1,0:T(8,128)S(1)}, f32[4,1,32,128]{3,2,1,0:T(8,128)S(1)}, u32[]{:S(2)}, u32[]{:S(2)}) collective-permute-start(f32[4,1,32,128]{3,2,1,0:T(8,128)S(1)} %get-tuple-element.79), channel_id=1, source_target_pairs={{8,0},{16,8},{24,16},{32,24},{40,32},{48,40},{56,48},{64,56},{72,6... | collective-permute-start | bytes 196616 | tf_op jit(solution)/shard_map/ppermute | solution.py:24
  13.8 5.4 %all-to-all-start.1 = ((bf16[32,4,3,128]{3,1,2,0:T(4,128)(2,1)}), bf16[32,4,3,128]{3,1,2,0:T(4,128)(2,1)S(1)}, u32[]{:S(2)}, u32[]{:S(2)}) async-start(bf16[32,4,3,128]{3,1,2,0:T(4,128)(2,1)} %copy.128), calls=%async_computation.1 | async-start | bytes 196608 | tf_op jit(solution)/shard_map/all_to_all | solution.py:124
  25.2 4.7 %collective-permute-start.2 = (f32[4,18,32,1]{2,1,3,0:T(8,128)S(1)}, f32[4,18,32,1]{2,1,3,0:T(8,128)S(1)}, u32[]{:S(2)}, u32[]{:S(2)}) collective-permute-start(f32[4,18,32,1]{2,1,3,0:T(8,128)S(1)} %copy.144), channel_id=1, source_target_pairs={{0,1},{1,2},{2,3},{3,4},{4,5},{5,6},{6,7},{8,9},{9,10},{10,11},{11... | collective-permute-start | bytes 27656 | tf_op jit(solution)/shard_map/ppermute | solution.py:21
  29.9 3.0 %broadcast_in_dim.21 = bf16[128,128,128]{2,1,0:T(8,128)(2,1)} broadcast(bf16[]{:T(256)} %constant.34.clone.1), dimensions={} | broadcast | bytes 4194306 | tf_op jit(solution)/shard_map/broadcast_in_dim | solution.py:107
  32.9 4.6 %scatter_fusion = bf16[128,128,128]{2,1,0:T(8,128)(2,1)} fusion(bf16[128,128,128]{2,1,0:T(8,128)(2,1)} %broadcast_in_dim.21, s32[32]{0:T(128)S(1)} %fusion.35, bf16[32,128,128]{2,1,0:T(8,128)(2,1)S(1)} %bitcast.58), kind=kCustom, calls=%fused_computation.1 | custom fusion | bytes 3145856 | tf_op jit(solution)/shard_map/scatter | solution.py:109
  40.5 3.2 %select_maximum_fusion = f32[4,18,34,130]{3,2,1,0:T(8,128)S(1)} fusion(f32[4,18,32,1]{3,2,1,0:T(8,128)} %copy.123, f32[4,18,32,128]{3,2,1,0:T(8,128)} %copy-done.1, f32[4,18,32,1]{3,2,1,0:T(8,128)} %copy.122), kind=kLoop, calls=%fused_computation.20 | loop fusion | flops 2545920 | bytes 2471040 | tf_op jit(solution)/shard_map/concatenate | solution.py:25
  45.1 2.5 %fusion.42 = (f32[3,17,34,130]{3,2,1,0:T(8,128)}, f32[3,17,34,130]{3,2,1,0:T(8,128)}) fusion(f32[4,18,34,130]{3,2,1,0:T(8,128)S(1)} %select_maximum_fusion), kind=kLoop, calls=%fused_computation.98 | loop fusion | bytes 3606720 | tf_op jit(solution)/shard_map/slice | solution.py:31
  49.6 7.4 %all-to-all-start = ((bf16[32,4,128,128]{3,2,1,0:T(8,128)(2,1)}), bf16[32,4,128,128]{3,2,1,0:T(8,128)(2,1)}, u32[]{:S(2)}, u32[]{:S(2)}) async-start(bf16[32,4,128,128]{3,2,1,0:T(8,128)(2,1)} %bitcast.53), calls=%async_computation | async-start | bytes 8388608 | tf_op jit(solution)/shard_map/all_to_all | solution.py:117
  57.1 2.8 %multiply_reduce_fusion.2 = f32[17,32,128]{2,1,0:T(8,128)S(1)} fusion(f32[3,17,34,130]{3,2,1,0:T(8,128)} %get-tuple-element.66, f32[3,17,34,130]{3,2,1,0:T(8,128)} %get-tuple-element.65), kind=kLoop, calls=%fused_computation.40 | loop fusion | flops 557056 | bytes 1949696 | tf_op jit(solution)/shard_map/reduce_sum | solution.py:41
  62.7 2.7 %broadcast_multiply_fusion.2 = f32[3,17,32,128]{3,2,1,0:T(8,128)S(1)} fusion(f32[17,32,128]{2,1,0:T(8,128)S(1)} %multiply_add_fusion.2, f32[3,17,34,130]{3,2,1,0:T(8,128)} %get-tuple-element.66, f32[3,17,34,130]{3,2,1,0:T(8,128)} %get-tuple-element.65), kind=kLoop, calls=%fused_computation.63 | loop fusion | flops 417792 | bytes 2785280 | tf_op jit(solution)/shard_map/mul | solution.py:48
  65.4 2.7 %broadcast_multiply_fusion.1 = f32[3,16,33,128]{3,2,1,0:T(8,128)S(1)} fusion(f32[16,33,128]{2,1,0:T(8,128)S(1)} %multiply_add_fusion.1, f32[3,18,33,130]{3,2,1,0:T(8,128)} %copy-done.3, f32[3,18,33,130]{3,2,1,0:T(8,128)} %copy-done.2), kind=kLoop, calls=%fused_computation.62 | loop fusion | flops 405504 | bytes 2703360 | tf_op jit(solution)/shard_map/mul | solution.py:48
  72.0 36.0 %all-to-all-done = bf16[32,4,128,128]{3,2,1,0:T(8,128)(2,1)} async-done(((bf16[32,4,128,128]{3,2,1,0:T(8,128)(2,1)}), bf16[32,4,128,128]{3,2,1,0:T(8,128)(2,1)}, u32[]{:S(2)}, u32[]{:S(2)}) %all-to-all-start) | async-done | bytes 4194336 | tf_op jit(solution)/shard_map/all_to_all | solution.py:117
  108.0 6.8 %fusion.13 = f32[128,3,128]{2,1,0:T(4,128)S(1)} fusion(bf16[128,128,128]{2,1,0:T(8,128)(2,1)} %bitcast.9, f32[128,3,128]{2,0,1:T(8,128)S(1)} %bitcast.57, bf16[128,3,128]{2,1,0:T(4,128)(2,1)S(1)} %gather_fusion, pred[128]{0:T(512)(128)(4,1)S(1)} %compare_and_fusion), kind=kOutput, calls=%fused_computation.32 | convolution fusion | flops 25313280 | bytes 4685952 | tf_op jit(solution)/shard_map/mij,mci->mcj/dot_general | solution.py:141
  115.0 4.9 %scatter_fusion.2 = f32[3,512,128]{2,0,1:T(4,128)S(1)} fusion(f32[3,512,128]{2,0,1:T(4,128)S(1)} %broadcast_in_dim.18, s32[128]{0:T(128)S(1)} %fusion.34, f32[128,3,128]{2,1,0:T(4,128)S(1)} %fusion.13), kind=kCustom, calls=%fused_computation.3 | custom fusion | flops 49152 | bytes 590336 | tf_op jit(solution)/shard_map/scatter-add | solution.py:147
  120.0 5.1 %collective-permute-start.5 = (f32[3,1,32,128]{3,2,1,0:T(8,128)S(1)}, f32[3,1,32,128]{3,2,1,0:T(8,128)S(1)}, u32[]{:S(2)}, u32[]{:S(2)}) collective-permute-start(f32[3,1,32,128]{3,2,1,0:T(8,128)S(1)} %get-tuple-element.82), channel_id=1, source_target_pairs={{8,0},{16,8},{24,16},{32,24},{40,32},{48,40},{56,48},{64,56},{72,6... | collective-permute-start | bytes 147464 | tf_op jit(solution)/shard_map/ppermute | solution.py:24
  127.1 2.2 %copy.135 = f32[3,16,32,128]{2,1,3,0:T(8,128)} copy(f32[3,16,32,128]{3,0,2,1:T(4,128)S(1)} %bitcast.55) | data formatting | bytes 1572864 | tf_op jit(solution)/shard_map/reshape | solution.py:149
  129.5 3.2 %collective-permute-done.4 = f32[3,1,32,128]{3,2,1,0:T(8,128)S(1)} collective-permute-done((f32[3,1,32,128]{3,2,1,0:T(8,128)S(1)}, f32[3,1,32,128]{3,2,1,0:T(8,128)S(1)}, u32[]{:S(2)}, u32[]{:S(2)}) %collective-permute-start.4) | collective-permute-done | bytes 49184 | tf_op jit(solution)/shard_map/ppermute | solution.py:21
  132.8 2.9 %pad_maximum_fusion = f32[3,18,32,128]{2,1,3,0:T(8,128)S(1)} fusion(f32[3,1,32,128]{2,1,3,0:T(1,128)S(1)} %copy.136, f32[3,16,32,128]{2,1,3,0:T(8,128)} %copy.135, f32[3,1,32,128]{2,1,3,0:T(1,128)S(1)} %copy.134), kind=kLoop, calls=%fused_computation.15 | loop fusion | flops 442368 | bytes 1769472 | tf_op jit(solution)/shard_map/concatenate | solution.py:25
  135.8 2.2 %copy-done = f32[3,18,32,128]{2,1,3,0:T(8,128)} copy-done((f32[3,18,32,128]{2,1,3,0:T(8,128)}, f32[3,18,32,128]{2,1,3,0:T(8,128)S(1)}, u32[]{:S(2)}) %copy-start) | copy-done | bytes 884760
  139.2 4.8 %collective-permute-start.6 = (f32[3,18,32,1]{2,1,3,0:T(8,128)S(1)}, f32[3,18,32,1]{2,1,3,0:T(8,128)S(1)}, u32[]{:S(2)}, u32[]{:S(2)}) collective-permute-start(f32[3,18,32,1]{2,1,3,0:T(8,128)S(1)} %get-tuple-element.63), channel_id=1, source_target_pairs={{0,1},{1,2},{2,3},{3,4},{4,5},{5,6},{6,7},{8,9},{9,10},{10,11},{11... | collective-permute-start | bytes 20744 | tf_op jit(solution)/shard_map/ppermute | solution.py:21
  146.2 4.5 %copy.138 = f32[3,18,32,128]{3,2,1,0:T(8,128)} copy(f32[3,18,32,128]{2,1,3,0:T(8,128)} %copy-done) | data formatting | bytes 1769472 | tf_op jit(solution)/shard_map/concatenate | solution.py:25
  151.5 2.1 %select_maximum_fusion.2 = f32[3,18,34,130]{3,2,1,0:T(8,128)S(1)} fusion(f32[3,18,32,1]{3,2,1,0:T(8,128)S(1)} %copy.139, f32[3,18,32,128]{3,2,1,0:T(8,128)} %copy.138, f32[3,18,32,1]{3,2,1,0:T(8,128)S(1)} %copy.137), kind=kLoop, calls=%fused_computation.23 | loop fusion | flops 1909440 | bytes 1853280 | tf_op jit(solution)/shard_map/concatenate | solution.py:25
  159.3 31.0 %while.11 = (s32[]{:T(128)}, f32[128]{0:T(128)S(1)}, f32[16,4096]{1,0:T(8,128)S(1)}, s32[16,4096]{1,0:T(8,128)}, s32[]{:T(128)}, /*index=5*/s32[]{:T(128)}) while((s32[]{:T(128)}, f32[128]{0:T(128)S(1)}, f32[16,4096]{1,0:T(8,128)S(1)}, s32[16,4096]{1,0:T(8,128)}, s32[]{:T(128)}, /*index=5*/s32[]{:T(128)}) %tuple.44), condition=%wide.region_9.10_spmd.clone, body=%wide.region_8.9_spmd.clone.sunk | while | flops 6816003 | bytes 66655 | solution.py:162
  190.3 19.1 %all-reduce.2 = f32[128]{0:T(128)S(1)} all-reduce(f32[128]{0:T(128)S(1)} %get-tuple-element.30), channel_id=2, replica_groups=mesh['fluid'=32,'wall'=8] {'wall'}, use_global_device_ids=true, to_apply=%region_10.11.clone | all-reduce | flops 128 | bytes 1024
  (134 shorter events, 69.0 us)
Async XLA Ops:
  1.5 18.7 %collective-permute-start = (f32[4,1,32,128]{3,2,1,0:T(8,128)S(1)}, f32[4,1,32,128]{3,2,1,0:T(8,128)S(1)}, u32[]{:S(2)}, u32[]{:S(2)}) collective-permute-start(f32[4,1,32,128]{3,2,1,0:T(8,128)S(1)} %get-tuple-element.80), channel_id=1, source_target_pairs={{0,8},{8,16},{16,24},{24,32},{32,40},{40,48},{48,56},{56,64},{64,7... | collective-permute-start | bytes 196616 | tf_op jit(solution)/shard_map/ppermute | solution.py:21
  3.4 18.1 %collective-permute-start.1 = (f32[4,1,32,128]{3,2,1,0:T(8,128)S(1)}, f32[4,1,32,128]{3,2,1,0:T(8,128)S(1)}, u32[]{:S(2)}, u32[]{:S(2)}) collective-permute-start(f32[4,1,32,128]{3,2,1,0:T(8,128)S(1)} %get-tuple-element.79), channel_id=1, source_target_pairs={{8,0},{16,8},{24,16},{32,24},{40,32},{48,40},{56,48},{64,56},{72,6... | collective-permute-start | bytes 196616 | tf_op jit(solution)/shard_map/ppermute | solution.py:24
  13.8 35.2 %all-to-all-start.1 = ((bf16[32,4,3,128]{3,1,2,0:T(4,128)(2,1)}), bf16[32,4,3,128]{3,1,2,0:T(4,128)(2,1)S(1)}, u32[]{:S(2)}, u32[]{:S(2)}) async-start(bf16[32,4,3,128]{3,1,2,0:T(4,128)(2,1)} %copy.128), calls=%async_computation.1 | async-start | bytes 196608 | tf_op jit(solution)/shard_map/all_to_all | solution.py:124
  21.6 1.0 copy-start.1
  23.2 14.2 %collective-permute-start.3 = (f32[4,18,32,1]{2,1,3,0:T(8,128)S(1)}, f32[4,18,32,1]{2,1,3,0:T(8,128)S(1)}, u32[]{:S(2)}, u32[]{:S(2)}) collective-permute-start(f32[4,18,32,1]{2,1,3,0:T(8,128)S(1)} %copy.145), channel_id=1, source_target_pairs={{1,0},{2,1},{3,2},{4,3},{5,4},{6,5},{7,6},{9,8},{10,9},{11,10},{12... | collective-permute-start | bytes 27656 | tf_op jit(solution)/shard_map/ppermute | solution.py:24
  25.2 7.7 %copy-start.11 = (bf16[1,1,32,128,128]{4,3,2,1,0:T(8,128)(2,1)S(1)}, bf16[1,1,32,128,128]{4,3,2,1,0:T(8,128)(2,1)}, u32[]{:S(2)}) copy-start(bf16[1,1,32,128,128]{4,3,2,1,0:T(8,128)(2,1)} %param.10) | copy-start | bytes 3145732
  25.2 13.9 %collective-permute-start.2 = (f32[4,18,32,1]{2,1,3,0:T(8,128)S(1)}, f32[4,18,32,1]{2,1,3,0:T(8,128)S(1)}, u32[]{:S(2)}, u32[]{:S(2)}) collective-permute-start(f32[4,18,32,1]{2,1,3,0:T(8,128)S(1)} %copy.144), channel_id=1, source_target_pairs={{0,1},{1,2},{2,3},{3,4},{4,5},{5,6},{6,7},{8,9},{9,10},{10,11},{11... | collective-permute-start | bytes 27656 | tf_op jit(solution)/shard_map/ppermute | solution.py:21
  45.1 2.6 %copy-start.2 = (f32[3,18,33,130]{3,2,1,0:T(8,128)}, f32[3,18,33,130]{3,2,1,0:T(8,128)S(1)}, u32[]{:S(2)}) copy-start(f32[3,18,33,130]{3,2,1,0:T(8,128)S(1)} %get-tuple-element.67) | copy-start | bytes 2779924
  45.1 3.3 %copy-start.3 = (f32[3,18,33,130]{3,2,1,0:T(8,128)}, f32[3,18,33,130]{3,2,1,0:T(8,128)S(1)}, u32[]{:S(2)}) copy-start(f32[3,18,33,130]{3,2,1,0:T(8,128)S(1)} %get-tuple-element.68) | copy-start | bytes 2779924
  49.6 58.3 %all-to-all-start = ((bf16[32,4,128,128]{3,2,1,0:T(8,128)(2,1)}), bf16[32,4,128,128]{3,2,1,0:T(8,128)(2,1)}, u32[]{:S(2)}, u32[]{:S(2)}) async-start(bf16[32,4,128,128]{3,2,1,0:T(8,128)(2,1)} %bitcast.53), calls=%async_computation | async-start | bytes 8388608 | tf_op jit(solution)/shard_map/all_to_all | solution.py:117
  57.1 2.8 %copy-start.10 = (f32[1,17,34,130]{3,2,1,0:T(8,128)S(1)}, f32[1,17,34,130]{3,2,1,0:T(8,128)}, u32[]{:S(2)}) copy-start(f32[1,17,34,130]{3,2,1,0:T(8,128)} %slice_subtract_fusion.14) | copy-start | bytes 901684
  60.3 2.4 %copy-start.8 = (f32[17,32,128]{2,1,0:T(8,128)}, f32[17,32,128]{2,1,0:T(8,128)S(1)}, u32[]{:S(2)}) copy-start(f32[17,32,128]{2,1,0:T(8,128)S(1)} %multiply_add_fusion.2) | copy-start | bytes 835588
  60.5 4.9 %copy-start.6 = (f32[16,33,128]{2,1,0:T(8,128)}, f32[16,33,128]{2,1,0:T(8,128)S(1)}, u32[]{:S(2)}) copy-start(f32[16,33,128]{2,1,0:T(8,128)S(1)} %multiply_add_fusion.1) | copy-start | bytes 811012
  68.1 1.2 copy-start.4
  69.4 2.5 %copy-start.13 = (bf16[32,4,3,128]{3,1,2,0:T(4,128)(2,1)S(1)}, bf16[32,4,3,128]{3,1,2,0:T(4,128)(2,1)}, u32[]{:S(2)}) copy-start(bf16[32,4,3,128]{3,1,2,0:T(4,128)(2,1)} %copy-done.12) | copy-start | bytes 294916
  120.0 9.3 %collective-permute-start.5 = (f32[3,1,32,128]{3,2,1,0:T(8,128)S(1)}, f32[3,1,32,128]{3,2,1,0:T(8,128)S(1)}, u32[]{:S(2)}, u32[]{:S(2)}) collective-permute-start(f32[3,1,32,128]{3,2,1,0:T(8,128)S(1)} %get-tuple-element.82), channel_id=1, source_target_pairs={{8,0},{16,8},{24,16},{32,24},{40,32},{48,40},{56,48},{64,56},{72,6... | collective-permute-start | bytes 147464 | tf_op jit(solution)/shard_map/ppermute | solution.py:24
  125.2 7.5 %collective-permute-start.4 = (f32[3,1,32,128]{3,2,1,0:T(8,128)S(1)}, f32[3,1,32,128]{3,2,1,0:T(8,128)S(1)}, u32[]{:S(2)}, u32[]{:S(2)}) collective-permute-start(f32[3,1,32,128]{3,2,1,0:T(8,128)S(1)} %get-tuple-element.81), channel_id=1, source_target_pairs={{0,8},{8,16},{16,24},{24,32},{32,40},{40,48},{48,56},{56,64},{64,7... | collective-permute-start | bytes 147464 | tf_op jit(solution)/shard_map/ppermute | solution.py:21
  132.8 11.2 %copy-start.14 = (s32[16,32,128]{2,1,0:T(8,128)S(1)}, s32[16,32,128]{2,1,0:T(8,128)}, u32[]{:S(2)}) copy-start(s32[16,32,128]{2,1,0:T(8,128)} %param.9) | copy-start | bytes 786436
  132.8 12.1 %copy-start.15 = (u32[256]{0:T(256)S(1)}, u32[256]{0:T(256)}, u32[]{:S(2)}) copy-start(u32[256]{0:T(256)} %constant.79) | copy-start | bytes 3076
  135.8 2.2 %copy-start = (f32[3,18,32,128]{2,1,3,0:T(8,128)}, f32[3,18,32,128]{2,1,3,0:T(8,128)S(1)}, u32[]{:S(2)}) copy-start(f32[3,18,32,128]{2,1,3,0:T(8,128)S(1)} %pad_maximum_fusion) | copy-start | bytes 2654212
  138.0 12.7 %collective-permute-start.7 = (f32[3,18,32,1]{2,1,3,0:T(8,128)S(1)}, f32[3,18,32,1]{2,1,3,0:T(8,128)S(1)}, u32[]{:S(2)}, u32[]{:S(2)}) collective-permute-start(f32[3,18,32,1]{2,1,3,0:T(8,128)S(1)} %get-tuple-element.64), channel_id=1, source_target_pairs={{1,0},{2,1},{3,2},{4,3},{5,4},{6,5},{7,6},{9,8},{10,9},{11,10},{12... | collective-permute-start | bytes 20744 | tf_op jit(solution)/shard_map/ppermute | solution.py:24
  139.2 11.8 %collective-permute-start.6 = (f32[3,18,32,1]{2,1,3,0:T(8,128)S(1)}, f32[3,18,32,1]{2,1,3,0:T(8,128)S(1)}, u32[]{:S(2)}, u32[]{:S(2)}) collective-permute-start(f32[3,18,32,1]{2,1,3,0:T(8,128)S(1)} %get-tuple-element.63), channel_id=1, source_target_pairs={{0,1},{1,2},{2,3},{3,4},{4,5},{5,6},{6,7},{8,9},{9,10},{10,11},{11... | collective-permute-start | bytes 20744 | tf_op jit(solution)/shard_map/ppermute | solution.py:21
  155.5 1.1 copy-start.9
  156.6 1.1 copy-start.5
  (2 other events, 1.6 us)
where the time goes:
time: 211 us; the launch traced here: 210 us
  local copies, waits for them, and re-layouts  55.3 us (26%)
  starting transfers between devices  39.6 us (19%)
  waiting for transfers between devices  39.2 us (19%)
  other arithmetic  31.8 us (15%)
  matrix products  22.7 us (11%)
  blocking collectives  19.1 us (9%)
    all_to_all x1, waiting for transfers between devices, body(): lax.all_to_all(send_tiles.reshape(block_groups, slot_limit, depth_width,...  36 us
    unnamed x1, blocking collectives  19.1 us
    dot_general x16, matrix products, add_slab(): jnp.dot(values, onehot, precision=lax.Precision.HIGHEST)  15.8 us
    dynamic_slice x16, local copies, waits for them, and re-layouts, body(): lax.scan(add_slab, jnp.zeros((reg_count,), jnp.float32), (product.reshape...  14.8 us
    ppermute x4, starting transfers between devices, with_halo(): lax.ppermute(lax.slice_in_dim(block, 0, width, axis=dim), axis, backward)  13.4 us
    ppermute x4, starting transfers between devices, with_halo(): lax.ppermute(lax.slice_in_dim(block, block.shape[dim] - width, None, axis...  13.3 us
    unnamed x40, local copies, waits for them, and re-layouts  11.1 us
    concatenate x3, other arithmetic, with_halo(): block = jnp.concatenate([low, block, high], axis=dim)  8.24 us
  transfers between devices with their start and end apart: 10, of which 2 were waited for; matrix products, arithmetic and copies ran while one was open for 24% of the time, Pallas kernels for 0%

commit v1 on v0

v1 whole, which is shorter than its diff:
```python
import functools

import jax
import jax.numpy as jnp
from jax import lax
from jax.experimental import pallas as pl
from jax.experimental.pallas import tpu as pltpu
from jax.sharding import PartitionSpec as P

CX, CY, TW = 16, 32, 128
CAP = 4
REG_DEV = 16
CELLS = CX * CY
TOP = 8
END = TOP + CY
ROWS = END + 8
MSG = 16

time_step = 0.12
nu_floor = 0.1
nu_spread = 0.9
relax_sq = 4.0
sens_scale = 0.03

MESH = pl.DeviceIdType.MESH
F32 = jnp.float32
BF16 = jnp.bfloat16


def iota(shape, dim):
    return lax.broadcasted_iota(jnp.int32, shape, dim)


def viscosity(jumps):
    base = 1.0 + relax_sq * (jumps[0] * jumps[0] + jumps[1] * jumps[1] + jumps[2] * jumps[2])
    root = lax.rsqrt(base)
    return nu_floor + nu_spread * (root * lax.rsqrt(root))


def pack_edges(planes, count, out_ref):
    half = ((iota((8, TW), 1) + 1) % TW) // 2

    def step(x, packed):
        packed = list(packed)
        for k in range(4):
            slot = 4 * x + k
            mine = half == slot
            for c in range(count):
                rows = planes[c, x + 1, TOP + 8 * k : TOP + 8 * k + 8, :]
                packed[c] = jnp.where(mine, pltpu.roll(rows, 2 * slot, 1), packed[c])
        return tuple(packed)

    packed = lax.fori_loop(0, CX, step, tuple(jnp.zeros((8, TW), F32) for _ in range(count)))
    for c in range(count):
        out_ref[c] = packed[c]


def packed_halo(low, high):
    even = iota((8, TW), 1) % 2 == 0
    return jnp.where(even, pltpu.roll(low, 1, 1), pltpu.roll(high, TW - 1, 1))


def unpack_edges(packed, x):
    rolled = [pltpu.roll(packed, (TW - 2 * (4 * x + k)) % TW, 1) for k in range(4)]
    lane = iota((CY, TW), 1)
    return jnp.where((lane == 0) | (lane == TW - 1), jnp.concatenate(rolled, axis=0), 0.0)


def kernel(
    nf, nw, tiles,
    flow, regions, obs, meas, dest, cells,
    vn_out, adj_out, sens_out,
    vp, fp, vn, adj, nux, nuy, nuz, nup, zo, zl, zh, fo, fl, fh,
    wts, reg, meas16, mask16, gat, gatt, route, obsv, sb, rb, mis, contrib, sb2, rb2, rhs,
    onelo, maskhi, prod, lhs, ps, pr,
    load_sem, store_sem, hs, hr, hs2, hr2, as1, ar1, as2, ar2, ws, wr,
):
    f = lax.axis_index("fluid")
    w = lax.axis_index("wall")
    barrier = pltpu.get_barrier_semaphore()
    for d in range(1, nf):
        pl.semaphore_signal(barrier, inc=1, device_id={"fluid": lax.rem(f + d, nf), "wall": w}, device_id_type=MESH)
    for d in range(1, nw):
        pl.semaphore_signal(barrier, inc=1, device_id={"fluid": f, "wall": lax.rem(w + d, nw)}, device_id_type=MESH)

    flow_loads = [
        pltpu.make_async_copy(flow.at[c], vp.at[c, 1 : CX + 1, TOP:END, :], load_sem.at[c]) for c in range(4)
    ]
    for load in flow_loads:
        load.start()
    reg_load = pltpu.make_async_copy(regions, reg, load_sem.at[4])
    reg_load.start()
    obs_load = pltpu.make_async_copy(obs, wts, load_sem.at[5])
    obs_load.start()

    def zero_pads(x, _):
        for c in range(4):
            vp[c, x + 1, 0:TOP, :] = jnp.zeros((TOP, TW), F32)
            vp[c, x + 1, END:ROWS, :] = jnp.zeros((ROWS - END, TW), F32)
        for c in range(3):
            fp[c, x + 1, 0:TOP, :] = jnp.zeros((TOP, TW), F32)
            fp[c, x + 1, END:ROWS, :] = jnp.zeros((ROWS - END, TW), F32)
        return 0

    lax.fori_loop(0, CX, zero_pads, 0)

    @pl.when(f == 0)
    def _():
        vp[:, 0, TOP:END, :] = jnp.zeros((4, CY, TW), F32)
        fp[:, 0, TOP:END, :] = jnp.zeros((3, CY, TW), F32)

    @pl.when(f == nf - 1)
    def _():
        vp[:, CX + 1, TOP:END, :] = jnp.zeros((4, CY, TW), F32)
        fp[:, CX + 1, TOP:END, :] = jnp.zeros((3, CY, TW), F32)

    @pl.when(w == 0)
    def _():
        zl[...] = jnp.zeros((4, 8, TW), F32)
        fl[...] = jnp.zeros((3, 8, TW), F32)

    @pl.when(w == nw - 1)
    def _():
        zh[...] = jnp.zeros((4, 8, TW), F32)
        fh[...] = jnp.zeros((3, 8, TW), F32)

    row16 = iota((MSG, TW), 0)
    lane16 = iota((MSG, TW), 1)
    slot16 = row16 // CAP
    comp16 = row16 % CAP

    def build_gather(p, _):
        ids = jnp.where(
            slot16 == 0, cells[p, 0], jnp.where(slot16 == 1, cells[p, 1], jnp.where(slot16 == 2, cells[p, 2], cells[p, 3]))
        )
        at = pl.ds(pl.multiple_of(p * MSG, MSG), MSG)
        for q in range(CELLS // TW):
            gat[at, q * TW : (q + 1) * TW] = jnp.where(ids == lane16 + q * TW, 1.0, 0.0).astype(BF16)
        return 0

    lax.fori_loop(0, nf, build_gather, 0)

    for load in flow_loads:
        load.wait()
    pack_edges(vp, 4, zo)

    pl.semaphore_wait(barrier, nf - 1 + nw - 1)

    def halo_copies(low_src, low_dst, high_src, high_dst, packed, from_low, from_high, ss, rr):
        up = pltpu.make_async_remote_copy(
            src_ref=high_src, dst_ref=low_dst, send_sem=ss.at[0], recv_sem=rr.at[0],
            device_id={"fluid": lax.rem(f + 1, nf), "wall": w}, device_id_type=MESH)
        down = pltpu.make_async_remote_copy(
            src_ref=low_src, dst_ref=high_dst, send_sem=ss.at[1], recv_sem=rr.at[1],
            device_id={"fluid": lax.rem(f + nf - 1, nf), "wall": w}, device_id_type=MESH)
        right = pltpu.make_async_remote_copy(
            src_ref=packed, dst_ref=from_low, send_sem=ss.at[2], recv_sem=rr.at[2],
            device_id={"fluid": f, "wall": lax.rem(w + 1, nw)}, device_id_type=MESH)
        left = pltpu.make_async_remote_copy(
            src_ref=packed, dst_ref=from_high, send_sem=ss.at[3], recv_sem=rr.at[3],
            device_id={"fluid": f, "wall": lax.rem(w + nw - 1, nw)}, device_id_type=MESH)
        return up, down, right, left

    def start_x(copies):
        pl.when(f < nf - 1)(copies[0].start)
        pl.when(f > 0)(copies[1].start)

    def start_z(copies):
        pl.when(w < nw - 1)(copies[2].start)
        pl.when(w > 0)(copies[3].start)

    def wait_halo(copies):
        pl.when(f > 0)(copies[0].wait_recv)
        pl.when(f < nf - 1)(copies[1].wait_recv)
        pl.when(w > 0)(copies[2].wait_recv)
        pl.when(w < nw - 1)(copies[3].wait_recv)

    def wait_halo_sent(copies):
        pl.when(f < nf - 1)(copies[0].wait_send)
        pl.when(f > 0)(copies[1].wait_send)
        pl.when(w < nw - 1)(copies[2].wait_send)
        pl.when(w > 0)(copies[3].wait_send)

    halo = halo_copies(
        flow.at[:, 0], vp.at[:, 0, TOP:END, :], flow.at[:, CX - 1], vp.at[:, CX + 1, TOP:END, :], zo, zl, zh, hs, hr)
    start_z(halo)
    start_x(halo)

    lane32 = iota((CY, TW), 1)
    first_lane = lane32 == 0
    last_lane = lane32 == TW - 1

    def forward_plane(x, carry, last):
        low_flux, low_p = carry[:3], carry[3]
        cur = [vp[c, x + 1, TOP:END, :] for c in range(4)]
        if last:
            flux_x = [jnp.zeros((CY, TW), F32) for _ in range(3)]
            high_p = jnp.zeros((CY, TW), F32)
        else:
            jump = [vp[c, x + 2, TOP:END, :] - cur[c] for c in range(3)]
            nu = viscosity(jump)
            nux[x + 1] = nu
            flux_x = [nu * j for j in jump]
            high_p = vp[3, x + 2, TOP:END, :]
        jump = [vp[c, x + 1, TOP:ROWS, :] - vp[c, x + 1, TOP - 1 : ROWS - 1, :] for c in range(3)]
        nu = viscosity(jump)
        nuy[x] = nu
        flux_y = [nu * j for j in jump]
        jump = [cur[c] - pltpu.roll(cur[c], 1, 1) for c in range(3)]
        nu = jnp.where(first_lane, 0.0, viscosity(jump))
        nuz[x] = nu
        flux_z = [nu * j for j in jump]
        grad = [
            high_p - low_p,
            vp[3, x + 1, TOP + 1 : END + 1, :] - vp[3, x + 1, TOP - 1 : END - 1, :],
            jnp.where(last_lane, 0.0, pltpu.roll(cur[3], TW - 1, 1)) - jnp.where(first_lane, 0.0, pltpu.roll(cur[3], 1, 1)),
        ]
        for c in range(3):
            div = (flux_x[c] - low_flux[c]) + (flux_y[c][1 : CY + 1] - flux_y[c][0:CY])
            div = div + (pltpu.roll(flux_z[c], TW - 1, 1) - flux_z[c])
            vn[c, x] = cur[c] + time_step * (div - 0.5 * grad[c])
        return (*flux_x, cur[3])

    start = tuple(jnp.zeros((CY, TW), F32) for _ in range(4))
    carry = lax.fori_loop(0, CX - 1, lambda x, carry: forward_plane(x, carry, False), start)
    forward_plane(CX - 1, carry, True)

    wait_halo(halo)
    for plane, ghost, face, sign in ((0, 0, 0, 1.0), (CX - 1, CX + 1, CX, -1.0)):
        jump = [vp[c, ghost, TOP:END, :] - vp[c, plane + 1, TOP:END, :] for c in range(3)]
        nu = viscosity(jump)
        nux[face] = nu
        for c in range(3):
            add = nu * jump[c]
            if c == 0:
                add = add + (0.5 * sign) * vp[3, ghost, TOP:END, :]
            vn[c, plane] = vn[c, plane] + time_step * add
    halo_p = packed_halo(zl[3], zh[3])
    jump = [packed_halo(zl[c], zh[c]) - zo[c] for c in range(3)]
    nu = viscosity(jump)
    nup[...] = nu
    even = iota((8, TW), 1) % 2 == 0
    fix = [time_step * nu * j for j in jump]
    fix[2] = fix[2] + jnp.where(even, 0.5 * time_step, -0.5 * time_step) * halo_p

    def finish_forward(x, _):
        at = pl.ds(pl.multiple_of(x * CY, CY), CY)
        for c in range(3):
            value = vn[c, x] + unpack_edges(fix[c], x)
            vn[c, x] = value
            obsv[at, c * TW : (c + 1) * TW] = value.astype(BF16)
        return 0

    lax.fori_loop(0, CX, finish_forward, 0)

    vn_store = pltpu.make_async_copy(vn, vn_out, store_sem.at[0])

    picked = jnp.dot(gat[...], obsv[...], preferred_element_type=F32)
    comp = iota((nf * MSG, TW), 0) % CAP
    message = jnp.where(
        comp == 0, picked[:, 0:TW],
        jnp.where(comp == 1, picked[:, TW : 2 * TW], jnp.where(comp == 2, picked[:, 2 * TW : 3 * TW], 0.0)),
    ).astype(BF16)
    sb[...] = message.reshape(nf, MSG, TW)

    def exchange(src, dst, ss, rr):
        def copy(peer, at):
            return pltpu.make_async_remote_copy(
                src_ref=src.at[peer], dst_ref=dst.at[at], send_sem=ss.at[peer], recv_sem=rr.at[at],
                device_id={"fluid": peer, "wall": w}, device_id_type=MESH)

        def send():
            def one(d, _):
                copy(lax.rem(f + d, nf), f).start()
                return 0

            lax.fori_loop(1, nf, one, 0)

        def receive():
            def one(d, _):
                peer = lax.rem(f + d, nf)
                copy(peer, peer).wait_recv()
                return 0

            lax.fori_loop(1, nf, one, 0)

        def sent():
            def one(d, _):
                peer = lax.rem(f + d, nf)
                copy(peer, peer).wait_send()
                return 0

            lax.fori_loop(1, nf, one, 0)

        return send, receive, sent

    send1, receive1, sent1 = exchange(sb, rb, as1, ar1)
    send2, receive2, sent2 = exchange(sb2, rb2, as2, ar2)
    send1()
    vn_store.start()
    rb[f] = sb[f]

    dest_lane = jnp.full((MSG, TW), -1, jnp.int32)
    for t in range(tiles):
        dest_lane = jnp.where(lane16 == t, dest[t], dest_lane)
    for t in range(tiles):
        earlier = jnp.where((dest_lane == dest[t]) & (lane16 < t), 1.0, 0.0)
        rank = jnp.sum(earlier, axis=1, keepdims=True)
        mask16[t] = jnp.where((slot16.astype(F32) == rank) & (comp16 < 3), 1.0, 0.0)
        rows = meas[t].astype(F32)
        meas16[t] = jnp.where(
            comp16 == 0, rows[0:1], jnp.where(comp16 == 1, rows[1:2], jnp.where(comp16 == 2, rows[2:3], 0.0)))
    own_row = (lane16 % MSG) == row16
    dest_of = []
    for q in range(tiles * MSG // TW):
        ids = jnp.full((MSG, TW), -1, jnp.int32)
        for u in range(TW // MSG):
            ids = jnp.where(own_row & (lane16 // MSG == u), dest[q * (TW // MSG) + u], ids)
        dest_of.append(ids)

    def build_route(b, _):
        at = pl.ds(pl.multiple_of(b * MSG, MSG), MSG)
        for q, ids in enumerate(dest_of):
            route[at, q * TW : (q + 1) * TW] = jnp.where(ids == b, 1.0, 0.0).astype(BF16)
        return 0

    lax.fori_loop(0, nf, build_route, 0)
    cell_of = []
    for q in range(nf * MSG // TW):
        ids = jnp.full((MSG, TW), -1, jnp.int32)
        for u in range(TW // MSG):
            for k in range(CAP):
                ids = jnp.where(lane16 // CAP == u * CAP + k, cells[q * (TW // MSG) + u, k], ids)
        cell_of.append(ids)

    def build_scatter(i, _):
        at = pl.ds(pl.multiple_of(i * MSG, MSG), MSG)
        for q, ids in enumerate(cell_of):
            gatt[at, q * TW : (q + 1) * TW] = jnp.where(ids == row16 + i * MSG, 1.0, 0.0).astype(BF16)
        return 0

    lax.fori_loop(0, CELLS // MSG, build_scatter, 0)

    obs_load.wait()
    receive1()
    for t in range(tiles):
        predicted = lax.dot_general(
            rb[dest[t]], wts[t], (((1,), (1,)), ((), ())), preferred_element_type=F32)
        mis[t] = ((predicted - meas16[t]) * mask16[t]).astype(BF16)
    for t in range(tiles):
        contrib[t * MSG : (t + 1) * MSG, :] = jnp.dot(mis[t], wts[t], preferred_element_type=F32).astype(BF16)
    sb2[...] = jnp.dot(route[...], contrib[...], preferred_element_type=F32).astype(BF16).reshape(nf, MSG, TW)
    send2()
    rb2[f] = sb2[f]

    reg_load.wait()
    row8 = iota((8, TW), 0)

    def build_regions(x, _):
        for y in range(CY):
            ids = jnp.broadcast_to(reg[x, y : y + 1, :], (MSG, TW))
            group = 2 * x + y // 16
            half, g = (y // 8) % 2, y % 8
            low = pl.multiple_of(group * TW + g * MSG, MSG)
            onelo[pl.ds(low, MSG), half * TW : (half + 1) * TW] = jnp.where(ids % REG_DEV == row16, 1.0, 0.0).astype(BF16)
            maskhi[x * CY + y] = jnp.where(ids[0:8] // REG_DEV == row8, 1.0, 0.0)
        return 0

    lax.fori_loop(0, CX, build_regions, 0)

    receive2()
    back = rb2[...].reshape(nf * MSG, TW).astype(F32)
    for c in range(3):
        rhs[:, c * TW : (c + 1) * TW] = jnp.where(comp == c, back, 0.0).astype(BF16)

    def force_rows(first, last):
        force = jnp.dot(gatt[first * CY : last * CY, :], rhs[...], preferred_element_type=F32)
        for x in range(first, last):
            for c in range(3):
                fp[c, x + 1, TOP:END, :] = force[(x - first) * CY : (x - first + 1) * CY, c * TW : (c + 1) * TW]

    force_rows(0, 1)
    force_rows(CX - 1, CX)
    halo2 = halo_copies(
        fp.at[:, 1, TOP:END, :], fp.at[:, 0, TOP:END, :], fp.at[:, CX, TOP:END, :], fp.at[:, CX + 1, TOP:END, :],
        fo, fl, fh, hs2, hr2)
    start_x(halo2)
    force_rows(1, CX - 1)
    pack_edges(fp, 3, fo)
    start_z(halo2)

    def adjoint_plane(x, carry, last):
        cur = [fp[c, x + 1, TOP:END, :] for c in range(3)]
        flux_x = []
        for c in range(3):
            if last:
                flux = jnp.zeros((CY, TW), F32)
            else:
                flux = nux[x + 1] * (fp[c, x + 2, TOP:END, :] - cur[c])
            flux_x.append(flux)
            flux_y = nuy[x] * (fp[c, x + 1, TOP:ROWS, :] - fp[c, x + 1, TOP - 1 : ROWS - 1, :])
            flux_z = nuz[x] * (cur[c] - pltpu.roll(cur[c], 1, 1))
            div = (flux - carry[c]) + (flux_y[1 : CY + 1] - flux_y[0:CY])
            div = div + (pltpu.roll(flux_z, TW - 1, 1) - flux_z)
            adj[c, x] = cur[c] + time_step * div
        return tuple(flux_x)

    carry = lax.fori_loop(0, CX - 1, lambda x, carry: adjoint_plane(x, carry, False), start[:3])
    adjoint_plane(CX - 1, carry, True)

    wait_halo(halo2)
    for plane, ghost, face in ((0, 0, 0), (CX - 1, CX + 1, CX)):
        for c in range(3):
            jump = fp[c, ghost, TOP:END, :] - fp[c, plane + 1, TOP:END, :]
            adj[c, plane] = adj[c, plane] + time_step * (nux[face] * jump)
    fix2 = [time_step * nup[...] * (packed_halo(fl[c], fh[c]) - fo[c]) for c in range(3)]

    def finish_adjoint(x, sums):
        total = jnp.zeros((CY, TW), F32)
        for c in range(3):
            value = adj[c, x] + unpack_edges(fix2[c], x)
            adj[c, x] = value
            total = total + value * vn[c, x]
        prod[...] = total
        for y in range(CY):
            half, g = (y // 8) % 2, y % 8
            row = (y // 16) * TW + g * MSG
            part = maskhi[x * CY + y] * jnp.broadcast_to(prod[y : y + 1, :], (8, TW))
            coarse = part.astype(BF16).astype(F32)
            lhs[row : row + MSG, half * TW : (half + 1) * TW] = jnp.concatenate(
                [coarse, part - coarse], axis=0).astype(BF16)
        for h in range(2):
            at = pl.ds(pl.multiple_of((2 * x + h) * TW, TW), TW)
            sums = sums + lax.dot_general(
                lhs[h * TW : (h + 1) * TW, :], onelo[at, :], (((1,), (1,)), ((), ())), preferred_element_type=F32)
        return sums

    sums = lax.fori_loop(0, CX, finish_adjoint, jnp.zeros((TW, TW), F32))
    adj_store = pltpu.make_async_copy(adj, adj_out, store_sem.at[1])
    adj_store.start()
    sums = jnp.where(iota((TW, TW), 0) // MSG == iota((TW, TW), 1) // MSG, sums, 0.0)
    short = sums[0:MSG]
    for g in range(1, TW // MSG):
        short = short + sums[g * MSG : (g + 1) * MSG]
    for shift in (64, 32, 16):
        short = short + pltpu.roll(short, shift, 1)
    owned = short[0:8] + short[8:16]
    ps[...] = owned

    def wall_copy(peer, at):
        return pltpu.make_async_remote_copy(
            src_ref=ps, dst_ref=pr.at[at], send_sem=ws.at[peer], recv_sem=wr.at[at],
            device_id={"fluid": f, "wall": peer}, device_id_type=MESH)

    for d in range(1, nw):
        wall_copy(lax.rem(w + d, nw), w).start()
    pr[w] = owned
    wait_halo_sent(halo)
    wait_halo_sent(halo2)
    sent1()
    sent2()
    for d in range(1, nw):
        peer = lax.rem(w + d, nw)
        wall_copy(peer, peer).wait_recv()
    total = pr[0]
    for p in range(1, nw):
        total = total + pr[p]
    mine = jnp.sum(jnp.where(row8 == w, total, 0.0), axis=0, keepdims=True)
    sens_out[...] = sens_scale * mine[:, 0:REG_DEV]
    for d in range(1, nw):
        peer = lax.rem(w + d, nw)
        wall_copy(peer, peer).wait_send()
    vn_store.wait()
    adj_store.wait()


def solution(mesh):
    nf, nw = mesh.shape["fluid"], mesh.shape["wall"]

    def body(flow_state, regions, obs_tiles, measured, tile_dest, cell_list):
        tiles = obs_tiles.shape[2]
        anywhere = pl.BlockSpec(memory_space=pl.ANY)
        in_vmem = pl.BlockSpec(memory_space=pltpu.VMEM)
        in_smem = pl.BlockSpec(memory_space=pltpu.SMEM)
        dma = pltpu.SemaphoreType.DMA
        msgs = nf * MSG
        vn, adj, sens = pl.pallas_call(
            functools.partial(kernel, nf, nw, tiles),
            out_shape=(
                jax.ShapeDtypeStruct((3, CX, CY, TW), F32),
                jax.ShapeDtypeStruct((3, CX, CY, TW), F32),
                jax.ShapeDtypeStruct((1, REG_DEV), F32),
            ),
            in_specs=[anywhere, anywhere, anywhere, in_vmem, in_smem, in_smem],
            out_specs=(anywhere, anywhere, in_vmem),
            scratch_shapes=[
                pltpu.VMEM((4, CX + 2, ROWS, TW), F32),
                pltpu.VMEM((3, CX + 2, ROWS, TW), F32),
                pltpu.VMEM((3, CX, CY, TW), F32),
                pltpu.VMEM((3, CX, CY, TW), F32),
                pltpu.VMEM((CX + 1, CY, TW), F32),
                pltpu.VMEM((CX, ROWS - TOP, TW), F32),
                pltpu.VMEM((CX, CY, TW), F32),
                pltpu.VMEM((8, TW), F32),
                pltpu.VMEM((4, 8, TW), F32),
                pltpu.VMEM((4, 8, TW), F32),
                pltpu.VMEM((4, 8, TW), F32),
                pltpu.VMEM((3, 8, TW), F32),
                pltpu.VMEM((3, 8, TW), F32),
                pltpu.VMEM((3, 8, TW), F32),
                pltpu.VMEM((tiles, TW, TW), BF16),
                pltpu.VMEM((CX, CY, TW), jnp.int32),
                pltpu.VMEM((tiles, MSG, TW), F32),
                pltpu.VMEM((tiles, MSG, TW), F32),
                pltpu.VMEM((msgs, CELLS), BF16),
                pltpu.VMEM((CELLS, msgs), BF16),
                pltpu.VMEM((msgs, tiles * MSG), BF16),
                pltpu.VMEM((CELLS, 3 * TW), BF16),
                pltpu.VMEM((nf, MSG, TW), BF16),
                pltpu.VMEM((nf, MSG, TW), BF16),
                pltpu.VMEM((tiles, MSG, TW), BF16),
                pltpu.VMEM((tiles * MSG, TW), BF16),
                pltpu.VMEM((nf, MSG, TW), BF16),
                pltpu.VMEM((nf, MSG, TW), BF16),
                pltpu.VMEM((msgs, 3 * TW), BF16),
                pltpu.VMEM((2 * CX * TW, 2 * TW), BF16),
                pltpu.VMEM((CELLS, 8, TW), F32),
                pltpu.VMEM((CY, TW), F32),
                pltpu.VMEM((2 * TW, 2 * TW), BF16),
                pltpu.VMEM((8, TW), F32),
                pltpu.VMEM((nw, 8, TW), F32),
                dma((6,)),
                dma((2,)),
                dma((4,)),
                dma((4,)),
                dma((4,)),
                dma((4,)),
                dma((nf,)),
                dma((nf,)),
                dma((nf,)),
                dma((nf,)),
                dma((nw,)),
                dma((nw,)),
            ],
            compiler_params=pltpu.CompilerParams(collective_id=0, has_side_effects=True),
        )(flow_state, regions, obs_tiles[0, 0], measured[0, 0], tile_dest[0, 0], cell_list[0, 0])
        return vn, adj, sens.reshape(REG_DEV)

    in_specs = (
        P(None, "fluid", None, "wall"),
        P("fluid", None, "wall"),
        P("fluid", "wall", None, None, None),
        P("fluid", "wall", None, None, None),
        P("fluid", "wall", None),
        P("fluid", "wall", None, None),
    )
    out_specs = (
        P(None, "fluid", None, "wall"),
        P(None, "fluid", None, "wall"),
        P(("fluid", "wall")),
    )
    return jax.shard_map(body, mesh=mesh, in_specs=in_specs, out_specs=out_specs, check_vma=False)
```

time: 211 us -> 51.4 us (0.24)
  local copies, waits for them, and re-layouts: 55.3 us -> 6.27 us
  Pallas kernels: 0 us -> 43.9 us
  starting transfers between devices: 39.6 us -> 0 us
  waiting for transfers between devices: 39.2 us -> 0 us
  other arithmetic: 31.8 us -> 0 us
  matrix products: 22.7 us -> 0 us
  blocking collectives: 19.1 us -> 0 us
    pallas_call x0 -> x1, Pallas kernels: none -> 43.9 us  [body(): pl.pallas_call(functools.partial(kernel, nf, nw, tiles), out_shape=(jax.S...]
    all_to_all x2 -> x0, waiting for transfers between devices: 36 us -> none  [the longest x1 36 us: body(): lax.all_to_all(send_tiles.reshape(block_groups, slot_limit, depth_width,...]
    ppermute x8 -> x0, starting transfers between devices: 26.7 us -> none  [the longest x4 13.4 us: with_halo(): lax.ppermute(lax.slice_in_dim(block, 0, width, axis=dim), axis, backward)]
    dot_general x17 -> x0, matrix products: 22.7 us -> none  [the longest x16 15.8 us: add_slab(): jnp.dot(values, onehot, precision=lax.Precision.HIGHEST)]
    unnamed x1 -> x0, blocking collectives: 19.1 us -> none
    dynamic_slice x16 -> x0, local copies, waits for them, and re-layouts: 14.8 us -> none  [body(): lax.scan(add_slab, jnp.zeros((reg_count,), jnp.float32), (product.reshape...]
    all_to_all x2 -> x0, starting transfers between devices: 12.9 us -> none  [the longest x1 7.43 us: body(): lax.all_to_all(send_tiles.reshape(block_groups, slot_limit, depth_width,...]
    mul x9 -> x0, other arithmetic: 8.54 us -> none  [the longest x6 7.47 us: divergence(): face_flux = nu_face[None] * face_jump]
  transfers between devices with their start and end apart: 10 -> 0, of which waited for: 2 -> 0; matrix products, arithmetic and copies ran while one was open for 24% -> 0% of each run, Pallas kernels for 0% -> 0%
where the time goes in v1:
time: 51.4 us; the launch traced here: 50.8 us
  Pallas kernels  43.9 us (85%)
  local copies, waits for them, and re-layouts  6.27 us (12%)
  between operations  0.66 us (1%)
    pallas_call x1, Pallas kernels, body(): pl.pallas_call(functools.partial(kernel, nf, nw, tiles), out_shape=(jax.S...  43.9 us
    unnamed x10, local copies, waits for them, and re-layouts  5.58 us

profile of v1, /device:TPU:8, one launch (start us, length us, event | category | flops | bytes accessed | tf_op | source)
XLA Modules:
  0.0 50.8 jit_solution(9334500501577346376)
XLA Ops:
  0.6 0.0 copy-start.1
  0.6 0.7 %copy-done.1 = s32[1,1,32,4]{2,3,1,0:T(4,128)S(1)} copy-done((s32[1,1,32,4]{2,3,1,0:T(4,128)S(1)}, s32[1,1,32,4]{2,3,1,0:T(4,128)}, u32[]{:S(2)}) %copy-start.1) | copy-done | bytes 536
  1.3 0.7 %copy.10.cells = s32[32,4]{1,0:T(8,128)} copy(s32[32,4]{0,1:T(4,128)S(1)} %bitcast.9) | data formatting | bytes 1024 | tf_op jit(solution)/shard_map/squeeze | solution.py:546
  2.0 1.4 %copy.12 = bf16[1,1,32,3,128]{4,3,2,1,0:T(4,128)(2,1)} copy(bf16[1,1,32,3,128]{4,2,3,1,0:T(8,128)(2,1)} %param.9) | data formatting | bytes 49152 | tf_op args[3]
  3.4 43.9 %shard_map.85 = (f32[3,16,32,128]{3,2,1,0:T(8,128)}, f32[3,16,32,128]{3,2,1,0:T(8,128)}, f32[1,16]{1,0:T(1,128)}) custom-call(f32[4,16,32,128]{3,2,1,0:T(8,128)} %flow.1, s32[16,32,128]{2,1,0:T(8,128)} %regions.1, bf16[32,128,128]{2,1,0:T(8,128)(2,1)} %bitcast.7, bf16[32,3,128]{2,1,0:T(4,128)(2,1)} %bitcast.8, s32[32]{0:T(128)} %bitcast.10, s32[32,4]{1,0:T(8,128)} %copy.10.cells), custom_call_target="tpu_custom_call" | custom-call | tf_op jit(solution)/shard_map/pallas_call | solution.py:487
  47.3 0.0 copy-start
  47.3 2.1 %copy.16 = f32[3,16,32,128]{3,2,1,0:T(8,128)} copy(f32[3,16,32,128]{3,2,1,0:T(8,128)} %get-tuple-element.12) | data formatting | bytes 1572864
  49.4 0.0 copy-done
  49.4 0.0 copy-start.2
  49.4 0.9 %copy.17 = f32[3,16,32,128]{3,2,1,0:T(8,128)} copy(f32[3,16,32,128]{3,2,1,0:T(8,128)S(1)} %copy-done) | data formatting | bytes 1572864
  50.3 0.0 copy-done.2
  50.3 0.5 %copy.18 = f32[16]{0:T(128)} copy(f32[16]{0:T(128)S(1)} %bitcast.11) | data formatting | bytes 128
Async XLA Ops:
  0.6 0.7 %copy-start.1 = (s32[1,1,32,4]{2,3,1,0:T(4,128)S(1)}, s32[1,1,32,4]{2,3,1,0:T(4,128)}, u32[]{:S(2)}) copy-start(s32[1,1,32,4]{2,3,1,0:T(4,128)} %param.11) | copy-start | bytes 1540
  47.3 2.1 %copy-start = (f32[3,16,32,128]{3,2,1,0:T(8,128)S(1)}, f32[3,16,32,128]{3,2,1,0:T(8,128)}, u32[]{:S(2)}) copy-start(f32[3,16,32,128]{3,2,1,0:T(8,128)} %get-tuple-element.13) | copy-start | bytes 2359300
  49.4 0.9 %copy-start.2 = (f32[1,16]{1,0:T(1,128)S(1)}, f32[1,16]{1,0:T(1,128)}, u32[]{:S(2)}) copy-start(f32[1,16]{1,0:T(1,128)} %get-tuple-element.8) | copy-start | bytes 196

commit v2 on v1

--- a/solution.py
+++ b/solution.py
@@ -37,22 +37,19 @@
     return nu_floor + nu_spread * (root * lax.rsqrt(root))
 
 
-def pack_edges(planes, count, out_ref):
+def pack_edges(rows_of, zero):
     half = ((iota((8, TW), 1) + 1) % TW) // 2
-
-    def step(x, packed):
-        packed = list(packed)
-        for k in range(4):
+    total = None
+    for k in range(4):
+        packed = zero
+        for x in range(CX):
             slot = 4 * x + k
-            mine = half == slot
-            for c in range(count):
-                rows = planes[c, x + 1, TOP + 8 * k : TOP + 8 * k + 8, :]
-                packed[c] = jnp.where(mine, pltpu.roll(rows, 2 * slot, 1), packed[c])
-        return tuple(packed)
-
-    packed = lax.fori_loop(0, CX, step, tuple(jnp.zeros((8, TW), F32) for _ in range(count)))
-    for c in range(count):
-        out_ref[c] = packed[c]
+            rows = rows_of(x, k)
+            if slot:
+                rows = pltpu.roll(rows, 2 * slot, 1)
+            packed = jnp.where(half == slot, rows, packed)
+        total = packed if total is None else total + packed
+    return total
 
 
 def packed_halo(low, high):
@@ -61,19 +58,46 @@
 
 
 def unpack_edges(packed, x):
-    rolled = [pltpu.roll(packed, (TW - 2 * (4 * x + k)) % TW, 1) for k in range(4)]
+    rolled = [pltpu.roll(packed, TW - 2 * (4 * x + k), 1) if x + k else packed for k in range(4)]
     lane = iota((CY, TW), 1)
     return jnp.where((lane == 0) | (lane == TW - 1), jnp.concatenate(rolled, axis=0), 0.0)
 
 
+def region_terms(values, masks):
+    parts = []
+    for value in values:
+        coarse = value.astype(BF16).astype(F32)
+        parts.append(jnp.concatenate([coarse, value - coarse], axis=0).astype(BF16))
+    rows = []
+    for h in range(8):
+        rows.append(jnp.concatenate([masks(k, h) * part for k, part in enumerate(parts)], axis=1))
+    return jnp.concatenate(rows, axis=0)
+
+
+def fine_labels(ids, store):
+    fine = ids % REG_DEV
+    for pair in range(REG_DEV // 2):
+        both = [jnp.where(fine == 2 * pair + i, 1.0, 0.0) for i in range(2)]
+        store(pair, jnp.concatenate(both, axis=0).astype(BF16))
+
+
+def coarse_mask(ids, h):
+    mask = jnp.where(ids // REG_DEV == h, 1.0, 0.0)
+    return jnp.concatenate([mask, mask], axis=0).astype(BF16)
+
+
+def contract_lanes(a, b):
+    return lax.dot_general(a, b, (((1,), (1,)), ((), ())), preferred_element_type=F32)
+
+
 def kernel(
     nf, nw, tiles,
-    flow, regions, obs, meas, dest, cells,
-    vn_out, adj_out, sens_out,
-    vp, fp, vn, adj, nux, nuy, nuz, nup, zo, zl, zh, fo, fl, fh,
+    flow, regions, obs, meas_in, dest_in, cells_in,
+    vn, adj, sens_out,
+    vp, fp, nux, nuy, nuz, nuzu, nup, vnp, zo, zl, zh, fo, fl, fh,
     wts, reg, meas16, mask16, gat, gatt, route, obsv, sb, rb, mis, contrib, sb2, rb2, rhs,
-    onelo, maskhi, prod, lhs, ps, pr,
-    load_sem, store_sem, hs, hr, hs2, hr2, as1, ar1, as2, ar2, ws, wr,
+    onelo, maskhi, onez, maskz, ps, pr, meas, dest, cells,
+    load_sem, hs, hr, hs2, hr2, as1, ar1, as2, ar2, ws, wr,
 ):
     f = lax.axis_index("fluid")
     w = lax.axis_index("wall")
@@ -91,58 +115,14 @@
     reg_load = pltpu.make_async_copy(regions, reg, load_sem.at[4])
     reg_load.start()
     obs_load = pltpu.make_async_copy(obs, wts, load_sem.at[5])
+    table_loads = [
+        pltpu.make_async_copy(cells_in, cells, load_sem.at[6]),
+        pltpu.make_async_copy(dest_in, dest, load_sem.at[7]),
+        pltpu.make_async_copy(meas_in, meas, load_sem.at[8]),
+    ]
+    for load in table_loads:
+        load.start()
     obs_load.start()
-
-    def zero_pads(x, _):
-        for c in range(4):
-            vp[c, x + 1, 0:TOP, :] = jnp.zeros((TOP, TW), F32)
-            vp[c, x + 1, END:ROWS, :] = jnp.zeros((ROWS - END, TW), F32)
-        for c in range(3):
-            fp[c, x + 1, 0:TOP, :] = jnp.zeros((TOP, TW), F32)
-            fp[c, x + 1, END:ROWS, :] = jnp.zeros((ROWS - END, TW), F32)
-        return 0
-
-    lax.fori_loop(0, CX, zero_pads, 0)
-
-    @pl.when(f == 0)
-    def _():
-        vp[:, 0, TOP:END, :] = jnp.zeros((4, CY, TW), F32)
-        fp[:, 0, TOP:END, :] = jnp.zeros((3, CY, TW), F32)
-
-    @pl.when(f == nf - 1)
-    def _():
-        vp[:, CX + 1, TOP:END, :] = jnp.zeros((4, CY, TW), F32)
-        fp[:, CX + 1, TOP:END, :] = jnp.zeros((3, CY, TW), F32)
-
-    @pl.when(w == 0)
-    def _():
-        zl[...] = jnp.zeros((4, 8, TW), F32)
-        fl[...] = jnp.zeros((3, 8, TW), F32)
-
-    @pl.when(w == nw - 1)
-    def _():
-        zh[...] = jnp.zeros((4, 8, TW), F32)
-        fh[...] = jnp.zeros((3, 8, TW), F32)
-
-    row16 = iota((MSG, TW), 0)
-    lane16 = iota((MSG, TW), 1)
-    slot16 = row16 // CAP
-    comp16 = row16 % CAP
-
-    def build_gather(p, _):
-        ids = jnp.where(
-            slot16 == 0, cells[p, 0], jnp.where(slot16 == 1, cells[p, 1], jnp.where(slot16 == 2, cells[p, 2], cells[p, 3]))
-        )
-        at = pl.ds(pl.multiple_of(p * MSG, MSG), MSG)
-        for q in range(CELLS // TW):
-            gat[at, q * TW : (q + 1) * TW] = jnp.where(ids == lane16 + q * TW, 1.0, 0.0).astype(BF16)
-        return 0
-
-    lax.fori_loop(0, nf, build_gather, 0)
-
-    for load in flow_loads:
-        load.wait()
-    pack_edges(vp, 4, zo)
 
     pl.semaphore_wait(barrier, nf - 1 + nw - 1)
 
@@ -183,8 +163,61 @@
 
     halo = halo_copies(
         flow.at[:, 0], vp.at[:, 0, TOP:END, :], flow.at[:, CX - 1], vp.at[:, CX + 1, TOP:END, :], zo, zl, zh, hs, hr)
+    start_x(halo)
+    for load in flow_loads:
+        load.wait()
+    for c in range(4):
+        zo[c] = pack_edges(lambda x, k: vp[c, x + 1, TOP + 8 * k : TOP + 8 * k + 8, :], jnp.zeros((8, TW), F32))
     start_z(halo)
-    start_x(halo)
+
+    @pl.when(f == 0)
+    def _():
+        vp[:, 0, TOP:END, :] = jnp.zeros((4, CY, TW), F32)
+        fp[:, 0, TOP:END, :] = jnp.zeros((3, CY, TW), F32)
+
+    @pl.when(f == nf - 1)
+    def _():
+        vp[:, CX + 1, TOP:END, :] = jnp.zeros((4, CY, TW), F32)
+        fp[:, CX + 1, TOP:END, :] = jnp.zeros((3, CY, TW), F32)
+
+    @pl.when(w == 0)
+    def _():
+        zl[...] = jnp.zeros((4, 8, TW), F32)
+        fl[...] = jnp.zeros((3, 8, TW), F32)
+
+    @pl.when(w == nw - 1)
+    def _():
+        zh[...] = jnp.zeros((4, 8, TW), F32)
+        fh[...] = jnp.zeros((3, 8, TW), F32)
+
+    def zero_pads(x, _):
+        for c in range(4):
+            vp[c, x + 1, 0:TOP, :] = jnp.zeros((TOP, TW), F32)
+            vp[c, x + 1, END:ROWS, :] = jnp.zeros((ROWS - END, TW), F32)
+        for c in range(3):
+            fp[c, x + 1, 0:TOP, :] = jnp.zeros((TOP, TW), F32)
+            fp[c, x + 1, END:ROWS, :] = jnp.zeros((ROWS - END, TW), F32)
+        return 0
+
+    lax.fori_loop(0, CX, zero_pads, 0)
+
+    row16 = iota((MSG, TW), 0)
+    lane16 = iota((MSG, TW), 1)
+    slot16 = row16 // CAP
+    comp16 = row16 % CAP
+
+    def build_gather(p, _):
+        ids = jnp.where(
+            slot16 == 0, cells[0, p], jnp.where(slot16 == 1, cells[1, p], jnp.where(slot16 == 2, cells[2, p], cells[3, p]))
+        )
+        at = pl.ds(pl.multiple_of(p * MSG, MSG), MSG)
+        for q in range(CELLS // TW):
+            gat[at, q * TW : (q + 1) * TW] = jnp.where(ids == lane16 + q * TW, 1.0, 0.0).astype(BF16)
+        return 0
+
+    for load in table_loads:
+        load.wait()
+    lax.fori_loop(0, nf, build_gather, 0)
 
     lane32 = iota((CY, TW), 1)
     first_lane = lane32 == 0
@@ -209,7 +242,9 @@
         jump = [cur[c] - pltpu.roll(cur[c], 1, 1) for c in range(3)]
         nu = jnp.where(first_lane, 0.0, viscosity(jump))
         nuz[x] = nu
-        flux_z = [nu * j for j in jump]
+        nu_up = pltpu.roll(nu, TW - 1, 1)
+        nuzu[x] = nu_up
+        flux_z = [nu_up * (pltpu.roll(cur[c], TW - 1, 1) - cur[c]) - nu * jump[c] for c in range(3)]
         grad = [
             high_p - low_p,
             vp[3, x + 1, TOP + 1 : END + 1, :] - vp[3, x + 1, TOP - 1 : END - 1, :],
@@ -217,12 +252,12 @@
         ]
         for c in range(3):
             div = (flux_x[c] - low_flux[c]) + (flux_y[c][1 : CY + 1] - flux_y[c][0:CY])
-            div = div + (pltpu.roll(flux_z[c], TW - 1, 1) - flux_z[c])
+            div = div + flux_z[c]
             vn[c, x] = cur[c] + time_step * (div - 0.5 * grad[c])
         return (*flux_x, cur[3])
 
     start = tuple(jnp.zeros((CY, TW), F32) for _ in range(4))
-    carry = lax.fori_loop(0, CX - 1, lambda x, carry: forward_plane(x, carry, False), start)
+    carry = lax.fori_loop(0, CX - 1, lambda x, carry: forward_plane(x, carry, False), start, unroll=3)
     forward_plane(CX - 1, carry, True)
 
     wait_halo(halo)
@@ -243,17 +278,11 @@
     fix = [time_step * nu * j for j in jump]
     fix[2] = fix[2] + jnp.where(even, 0.5 * time_step, -0.5 * time_step) * halo_p
 
-    def finish_forward(x, _):
-        at = pl.ds(pl.multiple_of(x * CY, CY), CY)
+    for x in range(CX):
         for c in range(3):
             value = vn[c, x] + unpack_edges(fix[c], x)
             vn[c, x] = value
-            obsv[at, c * TW : (c + 1) * TW] = value.astype(BF16)
-        return 0
-
-    lax.fori_loop(0, CX, finish_forward, 0)
-
-    vn_store = pltpu.make_async_copy(vn, vn_out, store_sem.at[0])
+            obsv[x * CY : (x + 1) * CY, c * TW : (c + 1) * TW] = value.astype(BF16)
 
     picked = jnp.dot(gat[...], obsv[...], preferred_element_type=F32)
     comp = iota((nf * MSG, TW), 0) % CAP
@@ -263,6 +292,12 @@
     ).astype(BF16)
     sb[...] = message.reshape(nf, MSG, TW)
 
+    def hops(d):
+        chip, side = d // 2, 4
+        return sum(min(at, side - at) for at in (chip % side, chip // side % side))
+
+    far_first = sorted(range(1, nf), key=lambda d: -hops(d))
+
     def exchange(src, dst, ss, rr):
         def copy(peer, at):
             return pltpu.make_async_remote_copy(
@@ -270,11 +305,8 @@
                 device_id={"fluid": peer, "wall": w}, device_id_type=MESH)
 
         def send():
-            def one(d, _):
+            for d in far_first:
                 copy(lax.rem(f + d, nf), f).start()
-                return 0
-
-            lax.fori_loop(1, nf, one, 0)
 
         def receive():
             def one(d, _):
@@ -297,9 +329,9 @@
     send1, receive1, sent1 = exchange(sb, rb, as1, ar1)
     send2, receive2, sent2 = exchange(sb2, rb2, as2, ar2)
     send1()
-    vn_store.start()
     rb[f] = sb[f]
 
+    by_tile = [meas[c].astype(F32) for c in range(3)]
     dest_lane = jnp.full((MSG, TW), -1, jnp.int32)
     for t in range(tiles):
         dest_lane = jnp.where(lane16 == t, dest[t], dest_lane)
@@ -307,9 +339,9 @@
         earlier = jnp.where((dest_lane == dest[t]) & (lane16 < t), 1.0, 0.0)
         rank = jnp.sum(earlier, axis=1, keepdims=True)
         mask16[t] = jnp.where((slot16.astype(F32) == rank) & (comp16 < 3), 1.0, 0.0)
-        rows = meas[t].astype(F32)
         meas16[t] = jnp.where(
-            comp16 == 0, rows[0:1], jnp.where(comp16 == 1, rows[1:2], jnp.where(comp16 == 2, rows[2:3], 0.0)))
+            comp16 == 0, by_tile[0][t : t + 1],
+            jnp.where(comp16 == 1, by_tile[1][t : t + 1], jnp.where(comp16 == 2, by_tile[2][t : t + 1], 0.0)))
     own_row = (lane16 % MSG) == row16
     dest_of = []
     for q in range(tiles * MSG // TW):
@@ -330,7 +362,7 @@
         ids = jnp.full((MSG, TW), -1, jnp.int32)
         for u in range(TW // MSG):
             for k in range(CAP):
-                ids = jnp.where(lane16 // CAP == u * CAP + k, cells[q * (TW // MSG) + u, k], ids)
+                ids = jnp.where(lane16 // CAP == u * CAP + k, cells[k, q * (TW // MSG) + u], ids)
         cell_of.append(ids)
 
     def build_scatter(i, _):
@@ -341,6 +373,30 @@
 
     lax.fori_loop(0, CELLS // MSG, build_scatter, 0)
 
+    reg_load.wait()
+
+    def build_regions(x, _):
+        at = pl.multiple_of(x * TW, TW)
+        for k in range(4):
+            ids = reg[x, 8 * k : 8 * k + 8, :]
+
+            def store(pair, rows, k=k):
+                onelo[pl.ds(at + MSG * pair, MSG), k * TW : (k + 1) * TW] = rows
+
+            fine_labels(ids, store)
+            for h in range(8):
+                maskhi[x, k, h] = coarse_mask(ids, h)
+        return 0
+
+    lax.fori_loop(0, CX, build_regions, 0)
+    packed_ids = pack_edges(lambda x, k: reg[x, 8 * k : 8 * k + 8, :], jnp.zeros((8, TW), jnp.int32))
+
+    def store_z(pair, rows):
+        onez[MSG * pair : MSG * pair + MSG, :] = rows
+
+    fine_labels(packed_ids, store_z)
+    for h in range(8):
+        maskz[h] = coarse_mask(packed_ids, h)
     obs_load.wait()
     receive1()
     for t in range(tiles):
@@ -353,21 +409,8 @@
     send2()
     rb2[f] = sb2[f]
 
-    reg_load.wait()
-    row8 = iota((8, TW), 0)
-
-    def build_regions(x, _):
-        for y in range(CY):
-            ids = jnp.broadcast_to(reg[x, y : y + 1, :], (MSG, TW))
-            group = 2 * x + y // 16
-            half, g = (y // 8) % 2, y % 8
-            low = pl.multiple_of(group * TW + g * MSG, MSG)
-            onelo[pl.ds(low, MSG), half * TW : (half + 1) * TW] = jnp.where(ids % REG_DEV == row16, 1.0, 0.0).astype(BF16)
-            maskhi[x * CY + y] = jnp.where(ids[0:8] // REG_DEV == row8, 1.0, 0.0)
-        return 0
-
-    lax.fori_loop(0, CX, build_regions, 0)
-
+    for c in range(3):
+        vnp[c] = pack_edges(lambda x, k: vn[c, x, 8 * k : 8 * k + 8, :], jnp.zeros((8, TW), F32))
     receive2()
     back = rb2[...].reshape(nf * MSG, TW).astype(F32)
     for c in range(3):
@@ -386,65 +429,59 @@
         fo, fl, fh, hs2, hr2)
     start_x(halo2)
     force_rows(1, CX - 1)
-    pack_edges(fp, 3, fo)
+    for c in range(3):
+        fo[c] = pack_edges(lambda x, k: fp[c, x + 1, TOP + 8 * k : TOP + 8 * k + 8, :], jnp.zeros((8, TW), F32))
     start_z(halo2)
 
+    def plane_sums(x, total):
+        at = pl.ds(pl.multiple_of(x * TW, TW), TW)
+        terms = region_terms([total[8 * k : 8 * k + 8] for k in range(4)], lambda k, h: maskhi[x, k, h])
+        return contract_lanes(terms, onelo[at, :])
+
     def adjoint_plane(x, carry, last):
-        cur = [fp[c, x + 1, TOP:END, :] for c in range(3)]
         flux_x = []
+        total = None
         for c in range(3):
+            cur = fp[c, x + 1, TOP:END, :]
             if last:
                 flux = jnp.zeros((CY, TW), F32)
             else:
-                flux = nux[x + 1] * (fp[c, x + 2, TOP:END, :] - cur[c])
+                flux = nux[x + 1] * (fp[c, x + 2, TOP:END, :] - cur)
             flux_x.append(flux)
-            flux_y = nuy[x] * (fp[c, x + 1, TOP:ROWS, :] - fp[c, x + 1, TOP - 1 : ROWS - 1, :])
-            flux_z = nuz[x] * (cur[c] - pltpu.roll(cur[c], 1, 1))
-            div = (flux - carry[c]) + (flux_y[1 : CY + 1] - flux_y[0:CY])
-            div = div + (pltpu.roll(flux_z, TW - 1, 1) - flux_z)
-            adj[c, x] = cur[c] + time_step * div
-        return tuple(flux_x)
-
-    carry = lax.fori_loop(0, CX - 1, lambda x, carry: adjoint_plane(x, carry, False), start[:3])
-    adjoint_plane(CX - 1, carry, True)
+            div = flux - carry[c]
+            div = div + nuy[x, 1 : CY + 1, :] * (fp[c, x + 1, TOP + 1 : END + 1, :] - cur)
+            div = div - nuy[x, 0:CY, :] * (cur - fp[c, x + 1, TOP - 1 : END - 1, :])
+            div = div + nuzu[x] * (pltpu.roll(cur, TW - 1, 1) - cur)
+            div = div - nuz[x] * (cur - pltpu.roll(cur, 1, 1))
+            value = cur + time_step * div
+            adj[c, x] = value
+            part = value * vn[c, x]
+            total = part if total is None else total + part
+        return (*flux_x, carry[3] + plane_sums(x, total))
+
+    carry = lax.fori_loop(
+        0, CX - 1, lambda x, carry: adjoint_plane(x, carry, False), (*start[:3], jnp.zeros((TW, TW), F32)), unroll=3)
+    sums = adjoint_plane(CX - 1, carry, True)[3]
 
     wait_halo(halo2)
+    fix2 = [time_step * nup[...] * (packed_halo(fl[c], fh[c]) - fo[c]) for c in range(3)]
+    total = fix2[0] * vnp[0] + fix2[1] * vnp[1] + fix2[2] * vnp[2]
+    sums = sums + contract_lanes(region_terms([total], lambda k, h: maskz[h]), onez[...])
     for plane, ghost, face in ((0, 0, 0), (CX - 1, CX + 1, CX)):
+        total = None
         for c in range(3):
             jump = fp[c, ghost, TOP:END, :] - fp[c, plane + 1, TOP:END, :]
-            adj[c, plane] = adj[c, plane] + time_step * (nux[face] * jump)
-    fix2 = [time_step * nup[...] * (packed_halo(fl[c], fh[c]) - fo[c]) for c in range(3)]
-
-    def finish_adjoint(x, sums):
-        total = jnp.zeros((CY, TW), F32)
-        for c in range(3):
-            value = adj[c, x] + unpack_edges(fix2[c], x)
-            adj[c, x] = value
-            total = total + value * vn[c, x]
-        prod[...] = total
-        for y in range(CY):
-            half, g = (y // 8) % 2, y % 8
-            row = (y // 16) * TW + g * MSG
-            part = maskhi[x * CY + y] * jnp.broadcast_to(prod[y : y + 1, :], (8, TW))
-            coarse = part.astype(BF16).astype(F32)
-            lhs[row : row + MSG, half * TW : (half + 1) * TW] = jnp.concatenate(
-                [coarse, part - coarse], axis=0).astype(BF16)
-        for h in range(2):
-            at = pl.ds(pl.multiple_of((2 * x + h) * TW, TW), TW)
-            sums = sums + lax.dot_general(
-                lhs[h * TW : (h + 1) * TW, :], onelo[at, :], (((1,), (1,)), ((), ())), preferred_element_type=F32)
-        return sums
-
-    sums = lax.fori_loop(0, CX, finish_adjoint, jnp.zeros((TW, TW), F32))
-    adj_store = pltpu.make_async_copy(adj, adj_out, store_sem.at[1])
-    adj_store.start()
-    sums = jnp.where(iota((TW, TW), 0) // MSG == iota((TW, TW), 1) // MSG, sums, 0.0)
-    short = sums[0:MSG]
-    for g in range(1, TW // MSG):
-        short = short + sums[g * MSG : (g + 1) * MSG]
-    for shift in (64, 32, 16):
-        short = short + pltpu.roll(short, shift, 1)
-    owned = short[0:8] + short[8:16]
+            value = time_step * (nux[face] * jump)
+            adj[c, plane] = adj[c, plane] + value
+            part = value * vn[c, plane]
+            total = part if total is None else total + part
+        sums = sums + plane_sums(plane, total)
+
+    sums = jnp.where(iota((TW, TW), 0) % 8 == iota((TW, TW), 1) % 8, sums, 0.0)
+    coarse_rows = [jnp.sum(sums[MSG * h : MSG * h + MSG], axis=0, keepdims=True) for h in range(8)]
+    pick = jnp.where(iota((TW, TW), 0) // 8 == iota((TW, TW), 1), 1.0, 0.0)
+    owned = jnp.dot(
+        jnp.concatenate(coarse_rows, axis=0), pick, precision=lax.Precision.HIGHEST, preferred_element_type=F32)
     ps[...] = owned
 
     def wall_copy(peer, at):
@@ -455,6 +492,9 @@
     for d in range(1, nw):
         wall_copy(lax.rem(w + d, nw), w).start()
     pr[w] = owned
+    for x in range(CX):
+        for c in range(3):
+            adj[c, x] = adj[c, x] + unpack_edges(fix2[c], x)
     wait_halo_sent(halo)
     wait_halo_sent(halo2)
     sent1()
@@ -465,13 +505,22 @@
     total = pr[0]
     for p in range(1, nw):
         total = total + pr[p]
-    mine = jnp.sum(jnp.where(row8 == w, total, 0.0), axis=0, keepdims=True)
+    mine = jnp.sum(jnp.where(iota((8, TW), 0) == w, total, 0.0), axis=0, keepdims=True)
     sens_out[...] = sens_scale * mine[:, 0:REG_DEV]
     for d in range(1, nw):
         peer = lax.rem(w + d, nw)
         wall_copy(peer, peer).wait_send()
-    vn_store.wait()
-    adj_store.wait()
+
+
+def write_out(vn, adj, sens, vn_out, adj_out, sens_out, sems):
+    copies = [
+        pltpu.make_async_copy(src, dst, sems.at[i])
+        for i, (src, dst) in enumerate(((vn, vn_out), (adj, adj_out), (sens, sens_out)))
+    ]
+    for copy in copies:
+        copy.start()
+    for copy in copies:
+        copy.wait()
 
 
 def solution(mesh):
@@ -479,29 +528,28 @@
 
     def body(flow_state, regions, obs_tiles, measured, tile_dest, cell_list):
         tiles = obs_tiles.shape[2]
-        anywhere = pl.BlockSpec(memory_space=pl.ANY)
+        in_hbm = pl.BlockSpec(memory_space=pltpu.HBM)
         in_vmem = pl.BlockSpec(memory_space=pltpu.VMEM)
-        in_smem = pl.BlockSpec(memory_space=pltpu.SMEM)
         dma = pltpu.SemaphoreType.DMA
         msgs = nf * MSG
         vn, adj, sens = pl.pallas_call(
             functools.partial(kernel, nf, nw, tiles),
             out_shape=(
-                jax.ShapeDtypeStruct((3, CX, CY, TW), F32),
-                jax.ShapeDtypeStruct((3, CX, CY, TW), F32),
-                jax.ShapeDtypeStruct((1, REG_DEV), F32),
+                pltpu.VMEM((3, CX, CY, TW), F32),
+                pltpu.VMEM((3, CX, CY, TW), F32),
+                pltpu.VMEM((1, REG_DEV), F32),
             ),
-            in_specs=[anywhere, anywhere, anywhere, in_vmem, in_smem, in_smem],
-            out_specs=(anywhere, anywhere, in_vmem),
+            in_specs=[in_hbm] * 6,
+            out_specs=(in_vmem, in_vmem, in_vmem),
             scratch_shapes=[
                 pltpu.VMEM((4, CX + 2, ROWS, TW), F32),
                 pltpu.VMEM((3, CX + 2, ROWS, TW), F32),
-                pltpu.VMEM((3, CX, CY, TW), F32),
-                pltpu.VMEM((3, CX, CY, TW), F32),
                 pltpu.VMEM((CX + 1, CY, TW), F32),
                 pltpu.VMEM((CX, ROWS - TOP, TW), F32),
                 pltpu.VMEM((CX, CY, TW), F32),
+                pltpu.VMEM((CX, CY, TW), F32),
                 pltpu.VMEM((8, TW), F32),
+                pltpu.VMEM((3, 8, TW), F32),
                 pltpu.VMEM((4, 8, TW), F32),
                 pltpu.VMEM((4, 8, TW), F32),
                 pltpu.VMEM((4, 8, TW), F32),
@@ -523,14 +571,16 @@
                 pltpu.VMEM((nf, MSG, TW), BF16),
                 pltpu.VMEM((nf, MSG, TW), BF16),
                 pltpu.VMEM((msgs, 3 * TW), BF16),
-                pltpu.VMEM((2 * CX * TW, 2 * TW), BF16),
-                pltpu.VMEM((CELLS, 8, TW), F32),
-                pltpu.VMEM((CY, TW), F32),
-                pltpu.VMEM((2 * TW, 2 * TW), BF16),
+                pltpu.VMEM((CX * TW, 4 * TW), BF16),
+                pltpu.VMEM((CX, 4, 8, MSG, TW), BF16),
+                pltpu.VMEM((TW, TW), BF16),
+                pltpu.VMEM((8, MSG, TW), BF16),
                 pltpu.VMEM((8, TW), F32),
                 pltpu.VMEM((nw, 8, TW), F32),
-                dma((6,)),
-                dma((2,)),
+                pltpu.VMEM((3, tiles, TW), BF16),
+                pltpu.SMEM((tiles,), jnp.int32),
+                pltpu.SMEM((CAP, nf), jnp.int32),
+                dma((9,)),
                 dma((4,)),
                 dma((4,)),
                 dma((4,)),
@@ -542,8 +592,19 @@
                 dma((nw,)),
                 dma((nw,)),
             ],
-            compiler_params=pltpu.CompilerParams(collective_id=0, has_side_effects=True),
-        )(flow_state, regions, obs_tiles[0, 0], measured[0, 0], tile_dest[0, 0], cell_list[0, 0])
+            compiler_params=pltpu.CompilerParams(collective_id=0, has_side_effects=True, vmem_limit_bytes=60 * 1024 * 1024),
+        )(
+            flow_state, regions, obs_tiles[0, 0], measured[0, 0].transpose(1, 0, 2), tile_dest[0, 0],
+            cell_list[0, 0].T,
+        )
+        vn, adj, sens = pl.pallas_call(
+            write_out,
+            out_shape=tuple(jax.ShapeDtypeStruct(a.shape, a.dtype) for a in (vn, adj, sens)),
+            in_specs=[in_vmem, in_vmem, in_vmem],
+            out_specs=(in_hbm, in_hbm, in_hbm),
+            scratch_shapes=[dma((3,))],
+            compiler_params=pltpu.CompilerParams(vmem_limit_bytes=8 << 20),
+        )(vn, adj, sens)
         return vn, adj, sens.reshape(REG_DEV)
 
     in_specs = (

time: 51.4 us -> 38.1 us (0.74)
  Pallas kernels: 43.9 us -> 37.1 us
  local copies, waits for them, and re-layouts: 6.27 us -> 0 us
    pallas_call x1 -> x2, Pallas kernels: 43.9 us -> 37.1 us  [the longest x1 36 us: body(): pl.pallas_call(functools.partial(kernel, nf, nw, tiles), out_shape=(pltpu...]
    unnamed x10 -> x0, local copies, waits for them, and re-layouts: 5.58 us -> none
    squeeze x1 -> x0, local copies, waits for them, and re-layouts: 0.69 us -> none  [body(): cell_list[0, 0]]
where the time goes in v2:
time: 38.1 us; the launch traced here: 37.8 us
  Pallas kernels  37.1 us (97%)
  between operations  0.64 us (2%)
    pallas_call x1, Pallas kernels, body(): pl.pallas_call(functools.partial(kernel, nf, nw, tiles), out_shape=(pltpu...  36 us
    pallas_call x1, Pallas kernels, body(): pl.pallas_call(write_out, out_shape=tuple((jax.ShapeDtypeStruct(a.shape,...  1.17 us

profile of v2, /device:TPU:8, one launch (start us, length us, event | category | flops | bytes accessed | tf_op | source)
XLA Modules:
  0.0 37.8 jit_solution(11830498324822283149)
XLA Ops:
  0.6 36.0 %shard_map.85 = (f32[3,16,32,128]{3,2,1,0:T(8,128)S(1)}, f32[3,16,32,128]{3,2,1,0:T(8,128)S(1)}, f32[1,16]{1,0:T(1,128)S(1)}) custom-call(f32[4,16,32,128]{3,2,1,0:T(8,128)} %flow.1, s32[16,32,128]{2,1,0:T(8,128)} %regions.1, bf16[32,128,128]{2,1,0:T(8,128)(2,1)} %bitcast.9, bf16[3,32,128]{2,1,0:T(8,128)(2,1)} %bitcast.10, s32[32]{0:T(128)} %bitcast.12, ...), custom_call_target="tpu_custom_call" | custom-call | tf_op jit(solution)/shard_map/pallas_call | solution.py:535
  36.6 1.2 %shard_map.86 = (f32[3,16,32,128]{3,2,1,0:T(8,128)}, f32[3,16,32,128]{3,2,1,0:T(8,128)}, f32[1,16]{1,0:T(1,128)}) custom-call(f32[3,16,32,128]{3,2,1,0:T(8,128)S(1)} %get-tuple-element.9.vn, f32[3,16,32,128]{3,2,1,0:T(8,128)S(1)} %get-tuple-element.10.adj, f32[1,16]{1,0:T(1,128)S(1)} %get-tuple-element.11.sens), custom_call_target="tpu_custom_call" | custom-call | tf_op jit(solution)/shard_map/pallas_call | solution.py:600

commit v3 on v2

--- a/solution.py
+++ b/solution.py
@@ -15,6 +15,7 @@
 END = TOP + CY
 ROWS = END + 8
 MSG = 16
+ROW = 8
 
 time_step = 0.12
 nu_floor = 0.1
@@ -64,26 +65,15 @@
 
 
 def region_terms(values, masks):
-    parts = []
-    for value in values:
-        coarse = value.astype(BF16).astype(F32)
-        parts.append(jnp.concatenate([coarse, value - coarse], axis=0).astype(BF16))
-    rows = []
-    for h in range(8):
-        rows.append(jnp.concatenate([masks(k, h) * part for k, part in enumerate(parts)], axis=1))
+    twice = [jnp.concatenate([value, value], axis=0).astype(BF16) for value in values]
+    rows = [jnp.concatenate([masks(k, pair) * v for k, v in enumerate(twice)], axis=1) for pair in range(4)]
     return jnp.concatenate(rows, axis=0)
 
 
-def fine_labels(ids, store):
-    fine = ids % REG_DEV
-    for pair in range(REG_DEV // 2):
-        both = [jnp.where(fine == 2 * pair + i, 1.0, 0.0) for i in range(2)]
+def label_pairs(labels, count, store):
+    for pair in range(count // 2):
+        both = [jnp.where(labels == 2 * pair + i, 1.0, 0.0) for i in range(2)]
         store(pair, jnp.concatenate(both, axis=0).astype(BF16))
-
-
-def coarse_mask(ids, h):
-    mask = jnp.where(ids // REG_DEV == h, 1.0, 0.0)
-    return jnp.concatenate([mask, mask], axis=0).astype(BF16)
 
 
 def contract_lanes(a, b):
@@ -95,26 +85,17 @@
     flow, regions, obs, meas_in, dest_in, cells_in,
     vn, adj, sens_out,
     vp, fp, nux, nuy, nuz, nuzu, nup, vnp, zo, zl, zh, fo, fl, fh,
-    wts, reg, meas16, mask16, gat, gatt, route, obsv, sb, rb, mis, contrib, sb2, rb2, rhs,
+    wts, reg, meas16, mask16, gat, gatt, route, obsv, big, sb, rb, mis, contrib, sb2, rb2, rhs,
     onelo, maskhi, onez, maskz, ps, pr, meas, dest, cells,
-    load_sem, hs, hr, hs2, hr2, as1, ar1, as2, ar2, ws, wr,
+    row_sem, wall_sem, load_sem, hs, hr, hs2, hr2, as1, ar1, as2, ar2, ws, wr,
 ):
     f = lax.axis_index("fluid")
     w = lax.axis_index("wall")
-    barrier = pltpu.get_barrier_semaphore()
-    for d in range(1, nf):
-        pl.semaphore_signal(barrier, inc=1, device_id={"fluid": lax.rem(f + d, nf), "wall": w}, device_id_type=MESH)
-    for d in range(1, nw):
-        pl.semaphore_signal(barrier, inc=1, device_id={"fluid": f, "wall": lax.rem(w + d, nw)}, device_id_type=MESH)
-
     flow_loads = [
         pltpu.make_async_copy(flow.at[c], vp.at[c, 1 : CX + 1, TOP:END, :], load_sem.at[c]) for c in range(4)
     ]
     for load in flow_loads:
         load.start()
-    reg_load = pltpu.make_async_copy(regions, reg, load_sem.at[4])
-    reg_load.start()
-    obs_load = pltpu.make_async_copy(obs, wts, load_sem.at[5])
     table_loads = [
         pltpu.make_async_copy(cells_in, cells, load_sem.at[6]),
         pltpu.make_async_copy(dest_in, dest, load_sem.at[7]),
@@ -122,9 +103,36 @@
     ]
     for load in table_loads:
         load.start()
-    obs_load.start()
-
-    pl.semaphore_wait(barrier, nf - 1 + nw - 1)
+
+    def signal(sem, to_f, to_w):
+        pl.semaphore_signal(
+            sem, inc=1, device_id={"fluid": lax.rem(to_f + nf, nf), "wall": lax.rem(to_w + nw, nw)}, device_id_type=MESH)
+
+    barrier = pltpu.get_barrier_semaphore()
+    many_rows = nf > ROW
+    row_start = (f // ROW) * ROW
+    near = [(f + 1, w), (f - 1, w), (f, w + 1), (f, w - 1)]
+    if many_rows:
+        near += [(f + ROW, w), (f - ROW, w)]
+    near += [(row_start + lax.rem(f + d, ROW), w) for d in range(1, ROW)]
+    for to_f, to_w in near:
+        signal(barrier, to_f, to_w)
+
+    def pass_rows(stage):
+        if many_rows:
+            signal(row_sem.at[stage], f + ROW, w)
+            signal(row_sem.at[stage], f - ROW, w)
+
+    def wait_rows(stage):
+        if many_rows:
+            pl.semaphore_wait(row_sem.at[stage], 2)
+
+    def pass_walls(stage):
+        signal(wall_sem.at[stage], f, w + 1)
+        signal(wall_sem.at[stage], f, w - 1)
+
+    def wait_walls(stage):
+        pl.semaphore_wait(wall_sem.at[stage], 2)
 
     def halo_copies(low_src, low_dst, high_src, high_dst, packed, from_low, from_high, ss, rr):
         up = pltpu.make_async_remote_copy(
@@ -161,15 +169,6 @@
         pl.when(w < nw - 1)(copies[2].wait_send)
         pl.when(w > 0)(copies[3].wait_send)
 
-    halo = halo_copies(
-        flow.at[:, 0], vp.at[:, 0, TOP:END, :], flow.at[:, CX - 1], vp.at[:, CX + 1, TOP:END, :], zo, zl, zh, hs, hr)
-    start_x(halo)
-    for load in flow_loads:
-        load.wait()
-    for c in range(4):
-        zo[c] = pack_edges(lambda x, k: vp[c, x + 1, TOP + 8 * k : TOP + 8 * k + 8, :], jnp.zeros((8, TW), F32))
-    start_z(halo)
-
     @pl.when(f == 0)
     def _():
         vp[:, 0, TOP:END, :] = jnp.zeros((4, CY, TW), F32)
@@ -206,18 +205,37 @@
     slot16 = row16 // CAP
     comp16 = row16 % CAP
 
-    def build_gather(p, _):
-        ids = jnp.where(
-            slot16 == 0, cells[0, p], jnp.where(slot16 == 1, cells[1, p], jnp.where(slot16 == 2, cells[2, p], cells[3, p]))
-        )
-        at = pl.ds(pl.multiple_of(p * MSG, MSG), MSG)
+    def build_gather(i, _):
+        ids = jnp.full((MSG, TW), -1, jnp.int32)
+        for u in range(MSG):
+            ids = jnp.where(row16 == u, cells[u % CAP, 4 * i + u // CAP], ids)
+        at = pl.ds(pl.multiple_of(i * MSG, MSG), MSG)
         for q in range(CELLS // TW):
             gat[at, q * TW : (q + 1) * TW] = jnp.where(ids == lane16 + q * TW, 1.0, 0.0).astype(BF16)
         return 0
 
+    big[...] = jnp.zeros((nf * MSG, TW), F32)
     for load in table_loads:
         load.wait()
-    lax.fori_loop(0, nf, build_gather, 0)
+    lax.fori_loop(0, nf // 4, build_gather, 0)
+
+    for load in flow_loads:
+        load.wait()
+    for c in range(4):
+        zo[c] = pack_edges(lambda x, k: vp[c, x + 1, TOP + 8 * k : TOP + 8 * k + 8, :], jnp.zeros((8, TW), F32))
+
+    reg_load = pltpu.make_async_copy(regions, reg, load_sem.at[4])
+    reg_load.start()
+    obs_load = pltpu.make_async_copy(obs, wts, load_sem.at[5])
+    obs_load.start()
+    halo = halo_copies(
+        vp.at[:, 1, TOP:END, :], vp.at[:, 0, TOP:END, :], vp.at[:, CX, TOP:END, :], vp.at[:, CX + 1, TOP:END, :],
+        zo, zl, zh, hs, hr)
+    pl.semaphore_wait(barrier, len(near))
+    start_x(halo)
+    start_z(halo)
+    pass_rows(0)
+    pass_walls(0)
 
     lane32 = iota((CY, TW), 1)
     first_lane = lane32 == 0
@@ -260,6 +278,10 @@
     carry = lax.fori_loop(0, CX - 1, lambda x, carry: forward_plane(x, carry, False), start, unroll=3)
     forward_plane(CX - 1, carry, True)
 
+    wait_rows(0)
+    pass_rows(1)
+    wait_walls(0)
+    pass_walls(1)
     wait_halo(halo)
     for plane, ghost, face, sign in ((0, 0, 0, 1.0), (CX - 1, CX + 1, CX, -1.0)):
         jump = [vp[c, ghost, TOP:END, :] - vp[c, plane + 1, TOP:END, :] for c in range(3)]
@@ -285,12 +307,9 @@
             obsv[x * CY : (x + 1) * CY, c * TW : (c + 1) * TW] = value.astype(BF16)
 
     picked = jnp.dot(gat[...], obsv[...], preferred_element_type=F32)
-    comp = iota((nf * MSG, TW), 0) % CAP
-    message = jnp.where(
-        comp == 0, picked[:, 0:TW],
-        jnp.where(comp == 1, picked[:, TW : 2 * TW], jnp.where(comp == 2, picked[:, 2 * TW : 3 * TW], 0.0)),
-    ).astype(BF16)
-    sb[...] = message.reshape(nf, MSG, TW)
+    for c in range(3):
+        big[pl.ds(c, nf * CAP, stride=CAP), :] = picked[:, c * TW : (c + 1) * TW]
+    sb[...] = big[...].astype(BF16).reshape(nf, MSG, TW)
 
     def hops(d):
         chip, side = d // 2, 4
@@ -309,12 +328,9 @@
                 copy(lax.rem(f + d, nf), f).start()
 
         def receive():
-            def one(d, _):
+            for d in reversed(far_first):
                 peer = lax.rem(f + d, nf)
                 copy(peer, peer).wait_recv()
-                return 0
-
-            lax.fori_loop(1, nf, one, 0)
 
         def sent():
             def one(d, _):
@@ -328,7 +344,10 @@
 
     send1, receive1, sent1 = exchange(sb, rb, as1, ar1)
     send2, receive2, sent2 = exchange(sb2, rb2, as2, ar2)
+    wait_rows(1)
     send1()
+    wait_walls(1)
+    pass_walls(2)
     rb[f] = sb[f]
 
     by_tile = [meas[c].astype(F32) for c in range(3)]
@@ -338,41 +357,29 @@
     for t in range(tiles):
         earlier = jnp.where((dest_lane == dest[t]) & (lane16 < t), 1.0, 0.0)
         rank = jnp.sum(earlier, axis=1, keepdims=True)
-        mask16[t] = jnp.where((slot16.astype(F32) == rank) & (comp16 < 3), 1.0, 0.0)
-        meas16[t] = jnp.where(
+        at_row, at_lane = MSG * (t % 2), TW * (t % 2)
+        blank = jnp.zeros((MSG, TW), F32)
+        mask16[t // 2, at_row : at_row + MSG, at_lane : at_lane + TW] = jnp.where(
+            (slot16.astype(F32) == rank) & (comp16 < 3), 1.0, 0.0)
+        mask16[t // 2, at_row : at_row + MSG, TW - at_lane : 2 * TW - at_lane] = blank
+        meas16[t // 2, at_row : at_row + MSG, TW - at_lane : 2 * TW - at_lane] = blank
+        meas16[t // 2, at_row : at_row + MSG, at_lane : at_lane + TW] = jnp.where(
             comp16 == 0, by_tile[0][t : t + 1],
             jnp.where(comp16 == 1, by_tile[1][t : t + 1], jnp.where(comp16 == 2, by_tile[2][t : t + 1], 0.0)))
-    own_row = (lane16 % MSG) == row16
-    dest_of = []
-    for q in range(tiles * MSG // TW):
-        ids = jnp.full((MSG, TW), -1, jnp.int32)
-        for u in range(TW // MSG):
-            ids = jnp.where(own_row & (lane16 // MSG == u), dest[q * (TW // MSG) + u], ids)
-        dest_of.append(ids)
-
-    def build_route(b, _):
-        at = pl.ds(pl.multiple_of(b * MSG, MSG), MSG)
-        for q, ids in enumerate(dest_of):
-            route[at, q * TW : (q + 1) * TW] = jnp.where(ids == b, 1.0, 0.0).astype(BF16)
-        return 0
-
-    lax.fori_loop(0, nf, build_route, 0)
-    cell_of = []
-    for q in range(nf * MSG // TW):
-        ids = jnp.full((MSG, TW), -1, jnp.int32)
-        for u in range(TW // MSG):
-            for k in range(CAP):
-                ids = jnp.where(lane16 // CAP == u * CAP + k, cells[k, q * (TW // MSG) + u], ids)
-        cell_of.append(ids)
+    route[...] = jnp.where(jnp.broadcast_to(dest_lane[0:1], (nf, TW)) == iota((nf, TW), 0), 1.0, 0.0).astype(BF16)
+    cell_of = jnp.full((MSG, TW), -1, jnp.int32)
+    for p in range(nf):
+        for k in range(CAP):
+            cell_of = jnp.where(lane16 == p * CAP + k, cells[k, p], cell_of)
 
     def build_scatter(i, _):
         at = pl.ds(pl.multiple_of(i * MSG, MSG), MSG)
-        for q, ids in enumerate(cell_of):
-            gatt[at, q * TW : (q + 1) * TW] = jnp.where(ids == row16 + i * MSG, 1.0, 0.0).astype(BF16)
+        gatt[at, :] = jnp.where(cell_of == row16 + i * MSG, 1.0, 0.0).astype(BF16)
         return 0
 
-    lax.fori_loop(0, CELLS // MSG, build_scatter, 0)
-
+    lax.fori_loop(0, CELLS // MSG, build_scatter, 0, unroll=4)
+    if nf * CAP < TW:
+        rhs[...] = jnp.zeros((TW, 3 * TW), BF16)
     reg_load.wait()
 
     def build_regions(x, _):
@@ -383,9 +390,12 @@
             def store(pair, rows, k=k):
                 onelo[pl.ds(at + MSG * pair, MSG), k * TW : (k + 1) * TW] = rows
 
-            fine_labels(ids, store)
-            for h in range(8):
-                maskhi[x, k, h] = coarse_mask(ids, h)
+            label_pairs(ids % REG_DEV, REG_DEV, store)
+
+            def store_mask(pair, rows, k=k):
+                maskhi[x, k, pair] = rows
+
+            label_pairs(ids // REG_DEV, 8, store_mask)
         return 0
 
     lax.fori_loop(0, CX, build_regions, 0)
@@ -394,27 +404,37 @@
     def store_z(pair, rows):
         onez[MSG * pair : MSG * pair + MSG, :] = rows
 
-    fine_labels(packed_ids, store_z)
-    for h in range(8):
-        maskz[h] = coarse_mask(packed_ids, h)
+    label_pairs(packed_ids % REG_DEV, REG_DEV, store_z)
+
+    def store_zmask(pair, rows):
+        maskz[pair] = rows
+
+    label_pairs(packed_ids // REG_DEV, 8, store_zmask)
     obs_load.wait()
     receive1()
-    for t in range(tiles):
-        predicted = lax.dot_general(
-            rb[dest[t]], wts[t], (((1,), (1,)), ((), ())), preferred_element_type=F32)
-        mis[t] = ((predicted - meas16[t]) * mask16[t]).astype(BF16)
-    for t in range(tiles):
-        contrib[t * MSG : (t + 1) * MSG, :] = jnp.dot(mis[t], wts[t], preferred_element_type=F32).astype(BF16)
-    sb2[...] = jnp.dot(route[...], contrib[...], preferred_element_type=F32).astype(BF16).reshape(nf, MSG, TW)
+    for p in range(tiles // 2):
+        pair = wts[2 * p : 2 * p + 2].reshape(2 * TW, TW)
+        predicted = contract_lanes(jnp.concatenate([rb[dest[2 * p]], rb[dest[2 * p + 1]]], axis=0), pair)
+        mis[p] = ((predicted - meas16[p]) * mask16[p]).astype(BF16)
+    for p in range(tiles // 2):
+        pair = wts[2 * p : 2 * p + 2].reshape(2 * TW, TW)
+        contrib[2 * p * MSG : 2 * (p + 1) * MSG, :] = jnp.dot(mis[p], pair, preferred_element_type=F32)
+    used = [r for r in range(MSG) if r % CAP < 3]
+    flat = jnp.concatenate([contrib[pl.ds(r, tiles, stride=MSG), :].astype(BF16) for r in used], axis=1)
+    routed = jnp.dot(route[:, 0:tiles], flat, preferred_element_type=F32)
+    for i, r in enumerate(used):
+        big[pl.ds(r, nf, stride=MSG), :] = routed[:, i * TW : (i + 1) * TW]
+    sb2[...] = big[...].astype(BF16).reshape(nf, MSG, TW)
     send2()
+    wait_walls(2)
     rb2[f] = sb2[f]
 
     for c in range(3):
         vnp[c] = pack_edges(lambda x, k: vn[c, x, 8 * k : 8 * k + 8, :], jnp.zeros((8, TW), F32))
     receive2()
-    back = rb2[...].reshape(nf * MSG, TW).astype(F32)
+    big[...] = rb2[...].reshape(nf * MSG, TW).astype(F32)
     for c in range(3):
-        rhs[:, c * TW : (c + 1) * TW] = jnp.where(comp == c, back, 0.0).astype(BF16)
+        rhs[0 : nf * CAP, c * TW : (c + 1) * TW] = big[pl.ds(c, nf * CAP, stride=CAP), :].astype(BF16)
 
     def force_rows(first, last):
         force = jnp.dot(gatt[first * CY : last * CY, :], rhs[...], preferred_element_type=F32)
@@ -460,7 +480,7 @@
         return (*flux_x, carry[3] + plane_sums(x, total))
 
     carry = lax.fori_loop(
-        0, CX - 1, lambda x, carry: adjoint_plane(x, carry, False), (*start[:3], jnp.zeros((TW, TW), F32)), unroll=3)
+        0, CX - 1, lambda x, carry: adjoint_plane(x, carry, False), (*start[:3], jnp.zeros((TW // 2, TW), F32)), unroll=3)
     sums = adjoint_plane(CX - 1, carry, True)[3]
 
     wait_halo(halo2)
@@ -477,8 +497,8 @@
             total = part if total is None else total + part
         sums = sums + plane_sums(plane, total)
 
-    sums = jnp.where(iota((TW, TW), 0) % 8 == iota((TW, TW), 1) % 8, sums, 0.0)
-    coarse_rows = [jnp.sum(sums[MSG * h : MSG * h + MSG], axis=0, keepdims=True) for h in range(8)]
+    sums = jnp.where(iota((TW // 2, TW), 0) % 8 == iota((TW // 2, TW), 1) % 8, sums, 0.0)
+    coarse_rows = [jnp.sum(sums[8 * h : 8 * h + 8], axis=0, keepdims=True) for h in range(8)]
     pick = jnp.where(iota((TW, TW), 0) // 8 == iota((TW, TW), 1), 1.0, 0.0)
     owned = jnp.dot(
         jnp.concatenate(coarse_rows, axis=0), pick, precision=lax.Precision.HIGHEST, preferred_element_type=F32)
@@ -531,7 +551,6 @@
         in_hbm = pl.BlockSpec(memory_space=pltpu.HBM)
         in_vmem = pl.BlockSpec(memory_space=pltpu.VMEM)
         dma = pltpu.SemaphoreType.DMA
-        msgs = nf * MSG
         vn, adj, sens = pl.pallas_call(
             functools.partial(kernel, nf, nw, tiles),
             out_shape=(
@@ -558,28 +577,31 @@
                 pltpu.VMEM((3, 8, TW), F32),
                 pltpu.VMEM((tiles, TW, TW), BF16),
                 pltpu.VMEM((CX, CY, TW), jnp.int32),
-                pltpu.VMEM((tiles, MSG, TW), F32),
-                pltpu.VMEM((tiles, MSG, TW), F32),
-                pltpu.VMEM((msgs, CELLS), BF16),
-                pltpu.VMEM((CELLS, msgs), BF16),
-                pltpu.VMEM((msgs, tiles * MSG), BF16),
+                pltpu.VMEM((tiles // 2, 2 * MSG, 2 * TW), F32),
+                pltpu.VMEM((tiles // 2, 2 * MSG, 2 * TW), F32),
+                pltpu.VMEM((nf * CAP, CELLS), BF16),
+                pltpu.VMEM((CELLS, TW), BF16),
+                pltpu.VMEM((nf, TW), BF16),
                 pltpu.VMEM((CELLS, 3 * TW), BF16),
+                pltpu.VMEM((nf * MSG, TW), F32),
                 pltpu.VMEM((nf, MSG, TW), BF16),
                 pltpu.VMEM((nf, MSG, TW), BF16),
-                pltpu.VMEM((tiles, MSG, TW), BF16),
-                pltpu.VMEM((tiles * MSG, TW), BF16),
+                pltpu.VMEM((tiles // 2, 2 * MSG, 2 * TW), BF16),
+                pltpu.VMEM((tiles * MSG, TW), F32),
                 pltpu.VMEM((nf, MSG, TW), BF16),
                 pltpu.VMEM((nf, MSG, TW), BF16),
-                pltpu.VMEM((msgs, 3 * TW), BF16),
+                pltpu.VMEM((TW, 3 * TW), BF16),
                 pltpu.VMEM((CX * TW, 4 * TW), BF16),
-                pltpu.VMEM((CX, 4, 8, MSG, TW), BF16),
+                pltpu.VMEM((CX, 4, 4, MSG, TW), BF16),
                 pltpu.VMEM((TW, TW), BF16),
-                pltpu.VMEM((8, MSG, TW), BF16),
+                pltpu.VMEM((4, MSG, TW), BF16),
                 pltpu.VMEM((8, TW), F32),
                 pltpu.VMEM((nw, 8, TW), F32),
                 pltpu.VMEM((3, tiles, TW), BF16),
                 pltpu.SMEM((tiles,), jnp.int32),
                 pltpu.SMEM((CAP, nf), jnp.int32),
+                pltpu.SemaphoreType.REGULAR((2,)),
+                pltpu.SemaphoreType.REGULAR((3,)),
                 dma((9,)),
                 dma((4,)),
                 dma((4,)),

time: 38.1 us -> 35.4 us (0.929)
  Pallas kernels: 37.1 us -> 34.4 us
    pallas_call x1, Pallas kernels: 36 us -> 33.3 us  [body(): pl.pallas_call(functools.partial(kernel, nf, nw, tiles), out_shape=(pltpu...]
where the time goes in v3:
time: 35.4 us; the launch traced here: 35.1 us
  Pallas kernels  34.4 us (97%)
  between operations  0.64 us (2%)
    pallas_call x1, Pallas kernels, body(): pl.pallas_call(functools.partial(kernel, nf, nw, tiles), out_shape=(pltpu...  33.3 us
    pallas_call x1, Pallas kernels, body(): pl.pallas_call(write_out, out_shape=tuple((jax.ShapeDtypeStruct(a.shape,...  1.17 us

profile of v3, /device:TPU:8, one launch (start us, length us, event | category | flops | bytes accessed | tf_op | source)
XLA Modules:
  0.0 35.1 jit_solution(317578291096431265)
XLA Ops:
  0.6 33.3 %shard_map.85 = (f32[3,16,32,128]{3,2,1,0:T(8,128)S(1)}, f32[3,16,32,128]{3,2,1,0:T(8,128)S(1)}, f32[1,16]{1,0:T(1,128)S(1)}) custom-call(f32[4,16,32,128]{3,2,1,0:T(8,128)} %flow.1, s32[16,32,128]{2,1,0:T(8,128)} %regions.1, bf16[32,128,128]{2,1,0:T(8,128)(2,1)} %bitcast.9, bf16[3,32,128]{2,1,0:T(8,128)(2,1)} %bitcast.10, s32[32]{0:T(128)} %bitcast.12, ...), custom_call_target="tpu_custom_call" | custom-call | tf_op jit(solution)/shard_map/pallas_call | solution.py:554
  33.9 1.2 %shard_map.86 = (f32[3,16,32,128]{3,2,1,0:T(8,128)}, f32[3,16,32,128]{3,2,1,0:T(8,128)}, f32[1,16]{1,0:T(1,128)}) custom-call(f32[3,16,32,128]{3,2,1,0:T(8,128)S(1)} %get-tuple-element.9.vn, f32[3,16,32,128]{3,2,1,0:T(8,128)S(1)} %get-tuple-element.10.adj, f32[1,16]{1,0:T(1,128)S(1)} %get-tuple-element.11.sens), custom_call_target="tpu_custom_call" | custom-call | tf_op jit(solution)/shard_map/pallas_call | solution.py:622

commit v4 on v3

--- a/solution.py
+++ b/solution.py
@@ -84,9 +84,9 @@
     nf, nw, tiles,
     flow, regions, obs, meas_in, dest_in, cells_in,
     vn, adj, sens_out,
-    vp, fp, nux, nuy, nuz, nuzu, nup, vnp, zo, zl, zh, fo, fl, fh,
+    vp, fp, hxs, hxr, fxs, fxr, nux, nuy, nuz, nuzu, nup, vnp, zo, zl, zh, fo, fl, fh,
     wts, reg, meas16, mask16, gat, gatt, route, obsv, big, sb, rb, mis, contrib, sb2, rb2, rhs,
-    onelo, maskhi, onez, maskz, ps, pr, meas, dest, cells,
+    onelo, maskhi, onez, maskz, pick, lhs, inner, ps, pr, meas, dest, cells,
     row_sem, wall_sem, load_sem, hs, hr, hs2, hr2, as1, ar1, as2, ar2, ws, wr,
 ):
     f = lax.axis_index("fluid")
@@ -111,20 +111,26 @@
     barrier = pltpu.get_barrier_semaphore()
     many_rows = nf > ROW
     row_start = (f // ROW) * ROW
+    in_row = lax.rem(f, ROW)
+    flip = 1 - 2 * lax.rem(f, 2)
+    beside = [row_start + lax.rem(in_row + d, ROW) for d in (2, ROW - 2)]
     near = [(f + 1, w), (f - 1, w), (f, w + 1), (f, w - 1)]
+    near += [(at, w) for at in beside] + [(at + flip, w) for at in beside] + [(f + flip, w)]
     if many_rows:
         near += [(f + ROW, w), (f - ROW, w)]
-    near += [(row_start + lax.rem(f + d, ROW), w) for d in range(1, ROW)]
     for to_f, to_w in near:
         signal(barrier, to_f, to_w)
 
     def pass_rows(stage):
-        if many_rows:
+        if stage == 0:
+            for at in beside:
+                signal(row_sem.at[0], at, w)
+        elif many_rows:
             signal(row_sem.at[stage], f + ROW, w)
             signal(row_sem.at[stage], f - ROW, w)
 
     def wait_rows(stage):
-        if many_rows:
+        if stage == 0 or many_rows:
             pl.semaphore_wait(row_sem.at[stage], 2)
 
     def pass_walls(stage):
@@ -171,13 +177,13 @@
 
     @pl.when(f == 0)
     def _():
-        vp[:, 0, TOP:END, :] = jnp.zeros((4, CY, TW), F32)
-        fp[:, 0, TOP:END, :] = jnp.zeros((3, CY, TW), F32)
+        hxr[0] = jnp.zeros((4, CY, TW), BF16)
+        fxr[0] = jnp.zeros((3, CY, TW), BF16)
 
     @pl.when(f == nf - 1)
     def _():
-        vp[:, CX + 1, TOP:END, :] = jnp.zeros((4, CY, TW), F32)
-        fp[:, CX + 1, TOP:END, :] = jnp.zeros((3, CY, TW), F32)
+        hxr[1] = jnp.zeros((4, CY, TW), BF16)
+        fxr[1] = jnp.zeros((3, CY, TW), BF16)
 
     @pl.when(w == 0)
     def _():
@@ -188,6 +194,20 @@
     def _():
         zh[...] = jnp.zeros((4, 8, TW), F32)
         fh[...] = jnp.zeros((3, 8, TW), F32)
+
+    row16 = iota((MSG, TW), 0)
+    lane16 = iota((MSG, TW), 1)
+    slot16 = row16 // CAP
+    comp16 = row16 % CAP
+
+    def build_gather(i, _):
+        ids = jnp.full((MSG, TW), -1, jnp.int32)
+        for u in range(MSG):
+            ids = jnp.where(row16 == u, cells[u % CAP, 4 * i + u // CAP], ids)
+        at = pl.ds(pl.multiple_of(i * MSG, MSG), MSG)
+        for q in range(CELLS // TW):
+            gat[at, q * TW : (q + 1) * TW] = jnp.where(ids == lane16 + q * TW, 1.0, 0.0).astype(BF16)
+        return 0
 
     def zero_pads(x, _):
         for c in range(4):
@@ -200,42 +220,26 @@
 
     lax.fori_loop(0, CX, zero_pads, 0)
 
-    row16 = iota((MSG, TW), 0)
-    lane16 = iota((MSG, TW), 1)
-    slot16 = row16 // CAP
-    comp16 = row16 % CAP
-
-    def build_gather(i, _):
-        ids = jnp.full((MSG, TW), -1, jnp.int32)
-        for u in range(MSG):
-            ids = jnp.where(row16 == u, cells[u % CAP, 4 * i + u // CAP], ids)
-        at = pl.ds(pl.multiple_of(i * MSG, MSG), MSG)
-        for q in range(CELLS // TW):
-            gat[at, q * TW : (q + 1) * TW] = jnp.where(ids == lane16 + q * TW, 1.0, 0.0).astype(BF16)
-        return 0
-
-    big[...] = jnp.zeros((nf * MSG, TW), F32)
-    for load in table_loads:
-        load.wait()
-    lax.fori_loop(0, nf // 4, build_gather, 0)
-
-    for load in flow_loads:
-        load.wait()
     for c in range(4):
+        flow_loads[c].wait()
+        hxs[0, c] = vp[c, 1, TOP:END, :].astype(BF16)
+        hxs[1, c] = vp[c, CX, TOP:END, :].astype(BF16)
         zo[c] = pack_edges(lambda x, k: vp[c, x + 1, TOP + 8 * k : TOP + 8 * k + 8, :], jnp.zeros((8, TW), F32))
-
-    reg_load = pltpu.make_async_copy(regions, reg, load_sem.at[4])
-    reg_load.start()
-    obs_load = pltpu.make_async_copy(obs, wts, load_sem.at[5])
-    obs_load.start()
     halo = halo_copies(
-        vp.at[:, 1, TOP:END, :], vp.at[:, 0, TOP:END, :], vp.at[:, CX, TOP:END, :], vp.at[:, CX + 1, TOP:END, :],
-        zo, zl, zh, hs, hr)
+        hxs.at[0], hxr.at[0], hxs.at[1], hxr.at[1], zo, zl, zh, hs, hr)
     pl.semaphore_wait(barrier, len(near))
     start_x(halo)
     start_z(halo)
     pass_rows(0)
     pass_walls(0)
+    reg_load = pltpu.make_async_copy(regions, reg, load_sem.at[4])
+    reg_load.start()
+    obs_load = pltpu.make_async_copy(obs, wts, load_sem.at[5])
+    obs_load.start()
+    big[...] = jnp.zeros((nf * MSG, TW), F32)
+    for load in table_loads:
+        load.wait()
+    lax.fori_loop(0, nf // 4, build_gather, 0)
 
     lane32 = iota((CY, TW), 1)
     first_lane = lane32 == 0
@@ -275,22 +279,26 @@
         return (*flux_x, cur[3])
 
     start = tuple(jnp.zeros((CY, TW), F32) for _ in range(4))
-    carry = lax.fori_loop(0, CX - 1, lambda x, carry: forward_plane(x, carry, False), start, unroll=3)
-    forward_plane(CX - 1, carry, True)
-
+    carry = lax.fori_loop(0, 9, lambda x, carry: forward_plane(x, carry, False), start, unroll=3)
     wait_rows(0)
     pass_rows(1)
+    carry = lax.fori_loop(9, CX - 1, lambda x, carry: forward_plane(x, carry, False), carry, unroll=3)
+    forward_plane(CX - 1, carry, True)
+
+    wait_rows(1)
+    pass_rows(2)
     wait_walls(0)
     pass_walls(1)
     wait_halo(halo)
-    for plane, ghost, face, sign in ((0, 0, 0, 1.0), (CX - 1, CX + 1, CX, -1.0)):
-        jump = [vp[c, ghost, TOP:END, :] - vp[c, plane + 1, TOP:END, :] for c in range(3)]
+    for plane, side, face, sign in ((0, 0, 0, 1.0), (CX - 1, 1, CX, -1.0)):
+        ghost = [hxr[side, c].astype(F32) for c in range(4)]
+        jump = [ghost[c] - vp[c, plane + 1, TOP:END, :] for c in range(3)]
         nu = viscosity(jump)
         nux[face] = nu
         for c in range(3):
             add = nu * jump[c]
             if c == 0:
-                add = add + (0.5 * sign) * vp[3, ghost, TOP:END, :]
+                add = add + (0.5 * sign) * ghost[3]
             vn[c, plane] = vn[c, plane] + time_step * add
     halo_p = packed_halo(zl[3], zh[3])
     jump = [packed_halo(zl[c], zh[c]) - zo[c] for c in range(3)]
@@ -344,7 +352,7 @@
 
     send1, receive1, sent1 = exchange(sb, rb, as1, ar1)
     send2, receive2, sent2 = exchange(sb2, rb2, as2, ar2)
-    wait_rows(1)
+    wait_rows(2)
     send1()
     wait_walls(1)
     pass_walls(2)
@@ -382,15 +390,16 @@
         rhs[...] = jnp.zeros((TW, 3 * TW), BF16)
     reg_load.wait()
 
+    label_of_lane = iota((TW, TW), 1) // 8
+
+    def by_fine_label(ids):
+        fine = jnp.concatenate([(ids % REG_DEV).astype(F32)] * REG_DEV, axis=0)
+        return jnp.where(fine.T == label_of_lane.astype(F32), 1.0, 0.0).astype(BF16)
+
     def build_regions(x, _):
-        at = pl.multiple_of(x * TW, TW)
         for k in range(4):
             ids = reg[x, 8 * k : 8 * k + 8, :]
-
-            def store(pair, rows, k=k):
-                onelo[pl.ds(at + MSG * pair, MSG), k * TW : (k + 1) * TW] = rows
-
-            label_pairs(ids % REG_DEV, REG_DEV, store)
+            onelo[pl.ds(pl.multiple_of((4 * x + k) * TW, TW), TW), :] = by_fine_label(ids)
 
             def store_mask(pair, rows, k=k):
                 maskhi[x, k, pair] = rows
@@ -401,15 +410,13 @@
     lax.fori_loop(0, CX, build_regions, 0)
     packed_ids = pack_edges(lambda x, k: reg[x, 8 * k : 8 * k + 8, :], jnp.zeros((8, TW), jnp.int32))
 
-    def store_z(pair, rows):
-        onez[MSG * pair : MSG * pair + MSG, :] = rows
-
-    label_pairs(packed_ids % REG_DEV, REG_DEV, store_z)
+    onez[...] = by_fine_label(packed_ids)
 
     def store_zmask(pair, rows):
         maskz[pair] = rows
 
     label_pairs(packed_ids // REG_DEV, 8, store_zmask)
+    pick[...] = jnp.where(iota((TW, TW), 0) // 8 == iota((TW, TW), 1), 1.0, 0.0).astype(BF16)
     obs_load.wait()
     receive1()
     for p in range(tiles // 2):
@@ -444,9 +451,11 @@
 
     force_rows(0, 1)
     force_rows(CX - 1, CX)
+    for c in range(3):
+        fxs[0, c] = fp[c, 1, TOP:END, :].astype(BF16)
+        fxs[1, c] = fp[c, CX, TOP:END, :].astype(BF16)
     halo2 = halo_copies(
-        fp.at[:, 1, TOP:END, :], fp.at[:, 0, TOP:END, :], fp.at[:, CX, TOP:END, :], fp.at[:, CX + 1, TOP:END, :],
-        fo, fl, fh, hs2, hr2)
+        fxs.at[0], fxr.at[0], fxs.at[1], fxr.at[1], fo, fl, fh, hs2, hr2)
     start_x(halo2)
     force_rows(1, CX - 1)
     for c in range(3):
@@ -454,9 +463,9 @@
     start_z(halo2)
 
     def plane_sums(x, total):
-        at = pl.ds(pl.multiple_of(x * TW, TW), TW)
+        at = pl.ds(pl.multiple_of(x * 4 * TW, TW), 4 * TW)
         terms = region_terms([total[8 * k : 8 * k + 8] for k in range(4)], lambda k, h: maskhi[x, k, h])
-        return contract_lanes(terms, onelo[at, :])
+        return jnp.dot(terms, onelo[at, :], preferred_element_type=F32)
 
     def adjoint_plane(x, carry, last):
         flux_x = []
@@ -477,20 +486,23 @@
             adj[c, x] = value
             part = value * vn[c, x]
             total = part if total is None else total + part
-        return (*flux_x, carry[3] + plane_sums(x, total))
-
-    carry = lax.fori_loop(
-        0, CX - 1, lambda x, carry: adjoint_plane(x, carry, False), (*start[:3], jnp.zeros((TW // 2, TW), F32)), unroll=3)
-    sums = adjoint_plane(CX - 1, carry, True)[3]
+        at = pl.ds(pl.multiple_of(x * 4 * TW, 4 * TW), 4 * TW)
+        lhs[:, at] = region_terms([total[8 * k : 8 * k + 8] for k in range(4)], lambda k, h: maskhi[x, k, h])
+        return tuple(flux_x)
+
+    carry = lax.fori_loop(0, CX - 1, lambda x, carry: adjoint_plane(x, carry, False), start[:3], unroll=3)
+    adjoint_plane(CX - 1, carry, True)
+    inner[...] = jnp.dot(lhs[...], onelo[...], preferred_element_type=F32)
 
     wait_halo(halo2)
     fix2 = [time_step * nup[...] * (packed_halo(fl[c], fh[c]) - fo[c]) for c in range(3)]
     total = fix2[0] * vnp[0] + fix2[1] * vnp[1] + fix2[2] * vnp[2]
-    sums = sums + contract_lanes(region_terms([total], lambda k, h: maskz[h]), onez[...])
-    for plane, ghost, face in ((0, 0, 0), (CX - 1, CX + 1, CX)):
+    terms = region_terms([total], lambda k, h: maskz[h])
+    sums = inner[...] + jnp.dot(terms, onez[...], preferred_element_type=F32)
+    for plane, side, face in ((0, 0, 0), (CX - 1, 1, CX)):
         total = None
         for c in range(3):
-            jump = fp[c, ghost, TOP:END, :] - fp[c, plane + 1, TOP:END, :]
+            jump = fxr[side, c].astype(F32) - fp[c, plane + 1, TOP:END, :]
             value = time_step * (nux[face] * jump)
             adj[c, plane] = adj[c, plane] + value
             part = value * vn[c, plane]
@@ -499,9 +511,14 @@
 
     sums = jnp.where(iota((TW // 2, TW), 0) % 8 == iota((TW // 2, TW), 1) % 8, sums, 0.0)
     coarse_rows = [jnp.sum(sums[8 * h : 8 * h + 8], axis=0, keepdims=True) for h in range(8)]
-    pick = jnp.where(iota((TW, TW), 0) // 8 == iota((TW, TW), 1), 1.0, 0.0)
-    owned = jnp.dot(
-        jnp.concatenate(coarse_rows, axis=0), pick, precision=lax.Precision.HIGHEST, preferred_element_type=F32)
+    by_label = jnp.concatenate(coarse_rows, axis=0)
+    parts = []
+    for _ in range(3):
+        part = by_label.astype(BF16)
+        parts.append(part)
+        by_label = by_label - part.astype(F32)
+    owned = jnp.dot(jnp.concatenate(parts, axis=0), pick[...], preferred_element_type=F32)
+    owned = owned[0:8] + owned[8:16] + owned[16:24]
     ps[...] = owned
 
     def wall_copy(peer, at):
@@ -509,7 +526,7 @@
             src_ref=ps, dst_ref=pr.at[at], send_sem=ws.at[peer], recv_sem=wr.at[at],
             device_id={"fluid": f, "wall": peer}, device_id_type=MESH)
 
-    for d in range(1, nw):
+    for d in sorted(range(1, nw), key=lambda d: -min(d, nw - d)):
         wall_copy(lax.rem(w + d, nw), w).start()
     pr[w] = owned
     for x in range(CX):
@@ -533,10 +550,10 @@
 
 
 def write_out(vn, adj, sens, vn_out, adj_out, sens_out, sems):
-    copies = [
-        pltpu.make_async_copy(src, dst, sems.at[i])
-        for i, (src, dst) in enumerate(((vn, vn_out), (adj, adj_out), (sens, sens_out)))
-    ]
+    copies = [pltpu.make_async_copy(sens, sens_out, sems.at[0])]
+    for c in range(3):
+        copies.append(pltpu.make_async_copy(vn.at[c], vn_out.at[c], sems.at[1 + c]))
+        copies.append(pltpu.make_async_copy(adj.at[c], adj_out.at[c], sems.at[4 + c]))
     for copy in copies:
         copy.start()
     for copy in copies:
@@ -563,6 +580,10 @@
             scratch_shapes=[
                 pltpu.VMEM((4, CX + 2, ROWS, TW), F32),
                 pltpu.VMEM((3, CX + 2, ROWS, TW), F32),
+                pltpu.VMEM((2, 4, CY, TW), BF16),
+                pltpu.VMEM((2, 4, CY, TW), BF16),
+                pltpu.VMEM((2, 3, CY, TW), BF16),
+                pltpu.VMEM((2, 3, CY, TW), BF16),
                 pltpu.VMEM((CX + 1, CY, TW), F32),
                 pltpu.VMEM((CX, ROWS - TOP, TW), F32),
                 pltpu.VMEM((CX, CY, TW), F32),
@@ -591,16 +612,19 @@
                 pltpu.VMEM((nf, MSG, TW), BF16),
                 pltpu.VMEM((nf, MSG, TW), BF16),
                 pltpu.VMEM((TW, 3 * TW), BF16),
-                pltpu.VMEM((CX * TW, 4 * TW), BF16),
+                pltpu.VMEM((CX * 4 * TW, TW), BF16),
                 pltpu.VMEM((CX, 4, 4, MSG, TW), BF16),
                 pltpu.VMEM((TW, TW), BF16),
                 pltpu.VMEM((4, MSG, TW), BF16),
+                pltpu.VMEM((TW, TW), BF16),
+                pltpu.VMEM((TW // 2, CX * 4 * TW), BF16),
+                pltpu.VMEM((TW // 2, TW), F32),
                 pltpu.VMEM((8, TW), F32),
                 pltpu.VMEM((nw, 8, TW), F32),
                 pltpu.VMEM((3, tiles, TW), BF16),
                 pltpu.SMEM((tiles,), jnp.int32),
                 pltpu.SMEM((CAP, nf), jnp.int32),
-                pltpu.SemaphoreType.REGULAR((2,)),
+                pltpu.SemaphoreType.REGULAR((3,)),
                 pltpu.SemaphoreType.REGULAR((3,)),
                 dma((9,)),
                 dma((4,)),
@@ -624,7 +648,7 @@
             out_shape=tuple(jax.ShapeDtypeStruct(a.shape, a.dtype) for a in (vn, adj, sens)),
             in_specs=[in_vmem, in_vmem, in_vmem],
             out_specs=(in_hbm, in_hbm, in_hbm),
-            scratch_shapes=[dma((3,))],
+            scratch_shapes=[dma((7,))],
             compiler_params=pltpu.CompilerParams(vmem_limit_bytes=8 << 20),
         )(vn, adj, sens)
         return vn, adj, sens.reshape(REG_DEV)

time: 35.4 us -> 35.3 us (level)
  no operation moved by 1% of the time
where the time goes in v4:
time: 35.3 us; the launch traced here: 35.2 us
  Pallas kernels  34.6 us (98%)
  between operations  0.64 us (2%)
    pallas_call x1, Pallas kernels, body(): pl.pallas_call(functools.partial(kernel, nf, nw, tiles), out_shape=(pltpu...  33.4 us
    pallas_call x1, Pallas kernels, body(): pl.pallas_call(write_out, out_shape=tuple((jax.ShapeDtypeStruct(a.shape,...  1.2 us

profile of v4, /device:TPU:8, one launch (start us, length us, event | category | flops | bytes accessed | tf_op | source)
XLA Modules:
  0.0 35.2 jit_solution(12944897342711675261)
XLA Ops:
  0.6 33.4 %shard_map.85 = (f32[3,16,32,128]{3,2,1,0:T(8,128)S(1)}, f32[3,16,32,128]{3,2,1,0:T(8,128)S(1)}, f32[1,16]{1,0:T(1,128)S(1)}) custom-call(f32[4,16,32,128]{3,2,1,0:T(8,128)} %flow.1, s32[16,32,128]{2,1,0:T(8,128)} %regions.1, bf16[32,128,128]{2,1,0:T(8,128)(2,1)} %bitcast.9, bf16[3,32,128]{2,1,0:T(8,128)(2,1)} %bitcast.10, s32[32]{0:T(128)} %bitcast.12, ...), custom_call_target="tpu_custom_call" | custom-call | tf_op jit(solution)/shard_map/pallas_call | solution.py:571
  34.0 1.2 %shard_map.86 = (f32[3,16,32,128]{3,2,1,0:T(8,128)}, f32[3,16,32,128]{3,2,1,0:T(8,128)}, f32[1,16]{1,0:T(1,128)}) custom-call(f32[3,16,32,128]{3,2,1,0:T(8,128)S(1)} %get-tuple-element.9.vn, f32[3,16,32,128]{3,2,1,0:T(8,128)S(1)} %get-tuple-element.10.adj, f32[1,16]{1,0:T(1,128)S(1)} %get-tuple-element.11.sens), custom_call_target="tpu_custom_call" | custom-call | tf_op jit(solution)/shard_map/pallas_call | solution.py:646

commit v5 on v4

--- a/solution.py
+++ b/solution.py
@@ -110,28 +110,29 @@
 
     barrier = pltpu.get_barrier_semaphore()
     many_rows = nf > ROW
-    row_start = (f // ROW) * ROW
     in_row = lax.rem(f, ROW)
     flip = 1 - 2 * lax.rem(f, 2)
-    beside = [row_start + lax.rem(in_row + d, ROW) for d in (2, ROW - 2)]
-    near = [(f + 1, w), (f - 1, w), (f, w + 1), (f, w - 1)]
-    near += [(at, w) for at in beside] + [(at + flip, w) for at in beside] + [(f + flip, w)]
+
+    def away(dx, dy):
+        return lax.rem((f // ROW + dy) * ROW + nf, nf) + lax.rem(in_row + 2 * dx + ROW, ROW)
+
+    beside = [away(1, 0), away(-1, 0)]
+    beyond = [away(2, 0)]
     if many_rows:
-        near += [(f + ROW, w), (f - ROW, w)]
+        beside += [away(0, 1), away(0, -1)]
+        beyond += [away(0, 2), away(1, 1), away(1, -1), away(-1, 1), away(-1, -1)]
+    near = [(f + 1, w), (f - 1, w), (f, w + 1), (f, w - 1), (f + flip, w)]
+    near += [(at, w) for at in beside] + [(at + flip, w) for at in beside]
     for to_f, to_w in near:
         signal(barrier, to_f, to_w)
+    rounds = (beside, beyond)
 
     def pass_rows(stage):
-        if stage == 0:
-            for at in beside:
-                signal(row_sem.at[0], at, w)
-        elif many_rows:
-            signal(row_sem.at[stage], f + ROW, w)
-            signal(row_sem.at[stage], f - ROW, w)
+        for at in rounds[stage]:
+            signal(row_sem.at[stage], at, w)
 
     def wait_rows(stage):
-        if stage == 0 or many_rows:
-            pl.semaphore_wait(row_sem.at[stage], 2)
+        pl.semaphore_wait(row_sem.at[stage], len(rounds[stage]))
 
     def pass_walls(stage):
         signal(wall_sem.at[stage], f, w + 1)
@@ -285,8 +286,6 @@
     carry = lax.fori_loop(9, CX - 1, lambda x, carry: forward_plane(x, carry, False), carry, unroll=3)
     forward_plane(CX - 1, carry, True)
 
-    wait_rows(1)
-    pass_rows(2)
     wait_walls(0)
     pass_walls(1)
     wait_halo(halo)
@@ -326,33 +325,21 @@
     far_first = sorted(range(1, nf), key=lambda d: -hops(d))
 
     def exchange(src, dst, ss, rr):
-        def copy(peer, at):
-            return pltpu.make_async_remote_copy(
-                src_ref=src.at[peer], dst_ref=dst.at[at], send_sem=ss.at[peer], recv_sem=rr.at[at],
-                device_id={"fluid": peer, "wall": w}, device_id_type=MESH)
-
         def send():
             for d in far_first:
-                copy(lax.rem(f + d, nf), f).start()
-
-        def receive():
-            for d in reversed(far_first):
                 peer = lax.rem(f + d, nf)
-                copy(peer, peer).wait_recv()
-
-        def sent():
-            def one(d, _):
-                peer = lax.rem(f + d, nf)
-                copy(peer, peer).wait_send()
-                return 0
-
-            lax.fori_loop(1, nf, one, 0)
-
-        return send, receive, sent
+                pltpu.make_async_remote_copy(
+                    src_ref=src.at[peer], dst_ref=dst.at[f], send_sem=ss, recv_sem=rr,
+                    device_id={"fluid": peer, "wall": w}, device_id_type=MESH).start()
+
+        every = pltpu.make_async_remote_copy(
+            src_ref=src.at[0 : nf - 1], dst_ref=dst.at[0 : nf - 1], send_sem=ss, recv_sem=rr,
+            device_id={"fluid": lax.rem(f + 1, nf), "wall": w}, device_id_type=MESH)
+        return send, every.wait_recv, every.wait_send
 
     send1, receive1, sent1 = exchange(sb, rb, as1, ar1)
     send2, receive2, sent2 = exchange(sb2, rb2, as2, ar2)
-    wait_rows(2)
+    wait_rows(1)
     send1()
     wait_walls(1)
     pass_walls(2)
@@ -382,7 +369,8 @@
 
     def build_scatter(i, _):
         at = pl.ds(pl.multiple_of(i * MSG, MSG), MSG)
-        gatt[at, :] = jnp.where(cell_of == row16 + i * MSG, 1.0, 0.0).astype(BF16)
+        first = jnp.where(i < 2, i * MSG, jnp.where(i < 4, (i + 2 * CX - 4) * MSG, (i - 2) * MSG))
+        gatt[at, :] = jnp.where(cell_of == row16 + first, 1.0, 0.0).astype(BF16)
         return 0
 
     lax.fori_loop(0, CELLS // MSG, build_scatter, 0, unroll=4)
@@ -443,21 +431,21 @@
     for c in range(3):
         rhs[0 : nf * CAP, c * TW : (c + 1) * TW] = big[pl.ds(c, nf * CAP, stride=CAP), :].astype(BF16)
 
-    def force_rows(first, last):
-        force = jnp.dot(gatt[first * CY : last * CY, :], rhs[...], preferred_element_type=F32)
-        for x in range(first, last):
+    def force_rows(first, planes):
+        rows = gatt[first * CY : (first + len(planes)) * CY, :]
+        force = jnp.dot(rows, rhs[...], preferred_element_type=F32)
+        for i, x in enumerate(planes):
             for c in range(3):
-                fp[c, x + 1, TOP:END, :] = force[(x - first) * CY : (x - first + 1) * CY, c * TW : (c + 1) * TW]
-
-    force_rows(0, 1)
-    force_rows(CX - 1, CX)
+                fp[c, x + 1, TOP:END, :] = force[i * CY : (i + 1) * CY, c * TW : (c + 1) * TW]
+
+    force_rows(0, (0, CX - 1))
     for c in range(3):
         fxs[0, c] = fp[c, 1, TOP:END, :].astype(BF16)
         fxs[1, c] = fp[c, CX, TOP:END, :].astype(BF16)
     halo2 = halo_copies(
         fxs.at[0], fxr.at[0], fxs.at[1], fxr.at[1], fo, fl, fh, hs2, hr2)
     start_x(halo2)
-    force_rows(1, CX - 1)
+    force_rows(2, range(1, CX - 1))
     for c in range(3):
         fo[c] = pack_edges(lambda x, k: fp[c, x + 1, TOP + 8 * k : TOP + 8 * k + 8, :], jnp.zeros((8, TW), F32))
     start_z(halo2)
@@ -519,15 +507,18 @@
         by_label = by_label - part.astype(F32)
     owned = jnp.dot(jnp.concatenate(parts, axis=0), pick[...], preferred_element_type=F32)
     owned = owned[0:8] + owned[8:16] + owned[16:24]
-    ps[...] = owned
-
-    def wall_copy(peer, at):
+    for p in range(nw):
+        ps[p] = owned
+
+    def wall_copy(peer, src, dst):
         return pltpu.make_async_remote_copy(
-            src_ref=ps, dst_ref=pr.at[at], send_sem=ws.at[peer], recv_sem=wr.at[at],
+            src_ref=src, dst_ref=dst, send_sem=ws, recv_sem=wr,
             device_id={"fluid": f, "wall": peer}, device_id_type=MESH)
 
+    every_wall = wall_copy(lax.rem(w + 1, nw), ps.at[0 : nw - 1], pr.at[0 : nw - 1])
     for d in sorted(range(1, nw), key=lambda d: -min(d, nw - d)):
-        wall_copy(lax.rem(w + d, nw), w).start()
+        peer = lax.rem(w + d, nw)
+        wall_copy(peer, ps.at[peer], pr.at[w]).start()
     pr[w] = owned
     for x in range(CX):
         for c in range(3):
@@ -536,17 +527,13 @@
     wait_halo_sent(halo2)
     sent1()
     sent2()
-    for d in range(1, nw):
-        peer = lax.rem(w + d, nw)
-        wall_copy(peer, peer).wait_recv()
+    every_wall.wait_recv()
     total = pr[0]
     for p in range(1, nw):
         total = total + pr[p]
     mine = jnp.sum(jnp.where(iota((8, TW), 0) == w, total, 0.0), axis=0, keepdims=True)
     sens_out[...] = sens_scale * mine[:, 0:REG_DEV]
-    for d in range(1, nw):
-        peer = lax.rem(w + d, nw)
-        wall_copy(peer, peer).wait_send()
+    every_wall.wait_send()
 
 
 def write_out(vn, adj, sens, vn_out, adj_out, sens_out, sems):
@@ -619,24 +606,24 @@
                 pltpu.VMEM((TW, TW), BF16),
                 pltpu.VMEM((TW // 2, CX * 4 * TW), BF16),
                 pltpu.VMEM((TW // 2, TW), F32),
-                pltpu.VMEM((8, TW), F32),
+                pltpu.VMEM((nw, 8, TW), F32),
                 pltpu.VMEM((nw, 8, TW), F32),
                 pltpu.VMEM((3, tiles, TW), BF16),
                 pltpu.SMEM((tiles,), jnp.int32),
                 pltpu.SMEM((CAP, nf), jnp.int32),
-                pltpu.SemaphoreType.REGULAR((3,)),
+                pltpu.SemaphoreType.REGULAR((2,)),
                 pltpu.SemaphoreType.REGULAR((3,)),
                 dma((9,)),
                 dma((4,)),
                 dma((4,)),
                 dma((4,)),
                 dma((4,)),
-                dma((nf,)),
-                dma((nf,)),
-                dma((nf,)),
-                dma((nf,)),
-                dma((nw,)),
-                dma((nw,)),
+                dma(()),
+                dma(()),
+                dma(()),
+                dma(()),
+                dma(()),
+                dma(()),
             ],
             compiler_params=pltpu.CompilerParams(collective_id=0, has_side_effects=True, vmem_limit_bytes=60 * 1024 * 1024),
         )(

time: 35.3 us -> 33.9 us (0.960); the launches traced: 35.2 us -> 33.4 us
  Pallas kernels: 34.6 us -> 32.8 us
    pallas_call x1, Pallas kernels: 33.4 us -> 31.6 us  [body(): pl.pallas_call(functools.partial(kernel, nf, nw, tiles), out_shape=(pltpu...]
where the time goes in v5:
time: 33.9 us; the launch traced here: 33.4 us
  Pallas kernels  32.8 us (97%)
  between operations  0.64 us (2%)
    pallas_call x1, Pallas kernels, body(): pl.pallas_call(functools.partial(kernel, nf, nw, tiles), out_shape=(pltpu...  31.6 us
    pallas_call x1, Pallas kernels, body(): pl.pallas_call(write_out, out_shape=tuple((jax.ShapeDtypeStruct(a.shape,...  1.2 us

profile of v5, /device:TPU:8, one launch (start us, length us, event | category | flops | bytes accessed | tf_op | source)
XLA Modules:
  0.0 33.4 jit_solution(1188913080618812960)
XLA Ops:
  0.6 31.6 %shard_map.85 = (f32[3,16,32,128]{3,2,1,0:T(8,128)S(1)}, f32[3,16,32,128]{3,2,1,0:T(8,128)S(1)}, f32[1,16]{1,0:T(1,128)S(1)}) custom-call(f32[4,16,32,128]{3,2,1,0:T(8,128)} %flow.1, s32[16,32,128]{2,1,0:T(8,128)} %regions.1, bf16[32,128,128]{2,1,0:T(8,128)(2,1)} %bitcast.9, bf16[3,32,128]{2,1,0:T(8,128)(2,1)} %bitcast.10, s32[32]{0:T(128)} %bitcast.12, ...), custom_call_target="tpu_custom_call" | custom-call | tf_op jit(solution)/shard_map/pallas_call | solution.py:558
  32.2 1.2 %shard_map.86 = (f32[3,16,32,128]{3,2,1,0:T(8,128)}, f32[3,16,32,128]{3,2,1,0:T(8,128)}, f32[1,16]{1,0:T(1,128)}) custom-call(f32[3,16,32,128]{3,2,1,0:T(8,128)S(1)} %get-tuple-element.9.vn, f32[3,16,32,128]{3,2,1,0:T(8,128)S(1)} %get-tuple-element.10.adj, f32[1,16]{1,0:T(1,128)S(1)} %get-tuple-element.11.sens), custom_call_target="tpu_custom_call" | custom-call | tf_op jit(solution)/shard_map/pallas_call | solution.py:633

commit v6 on v5

--- a/solution.py
+++ b/solution.py
@@ -121,10 +121,13 @@
     if many_rows:
         beside += [away(0, 1), away(0, -1)]
         beyond += [away(0, 2), away(1, 1), away(1, -1), away(-1, 1), away(-1, -1)]
-    near = [(f + 1, w), (f - 1, w), (f, w + 1), (f, w - 1), (f + flip, w)]
+    near = [(f, w + 1), (f, w - 1), (f + flip, w)]
     near += [(at, w) for at in beside] + [(at + flip, w) for at in beside]
+    pl.when(f < nf - 1)(lambda: signal(barrier, f + 1, w))
+    pl.when(f > 0)(lambda: signal(barrier, f - 1, w))
     for to_f, to_w in near:
         signal(barrier, to_f, to_w)
+    expected = len(near) + (f + nf - 1) // nf + (2 * nf - 2 - f) // nf
     rounds = (beside, beyond)
 
     def pass_rows(stage):
@@ -228,7 +231,7 @@
         zo[c] = pack_edges(lambda x, k: vp[c, x + 1, TOP + 8 * k : TOP + 8 * k + 8, :], jnp.zeros((8, TW), F32))
     halo = halo_copies(
         hxs.at[0], hxr.at[0], hxs.at[1], hxr.at[1], zo, zl, zh, hs, hr)
-    pl.semaphore_wait(barrier, len(near))
+    pl.semaphore_wait(barrier, expected)
     start_x(halo)
     start_z(halo)
     pass_rows(0)

time: 33.9 us -> 33.5 us (0.988)
  no operation moved by 1% of the time
where the time goes in v6:
time: 33.5 us; the launch traced here: 33.2 us
  Pallas kernels  32.5 us (97%)
  between operations  0.64 us (2%)
    pallas_call x1, Pallas kernels, body(): pl.pallas_call(functools.partial(kernel, nf, nw, tiles), out_shape=(pltpu...  31.3 us
    pallas_call x1, Pallas kernels, body(): pl.pallas_call(write_out, out_shape=tuple((jax.ShapeDtypeStruct(a.shape,...  1.2 us

profile of v6, /device:TPU:8, one launch (start us, length us, event | category | flops | bytes accessed | tf_op | source)
XLA Modules:
  0.0 33.2 jit_solution(7602876348443659199)
XLA Ops:
  0.6 31.3 %shard_map.85 = (f32[3,16,32,128]{3,2,1,0:T(8,128)S(1)}, f32[3,16,32,128]{3,2,1,0:T(8,128)S(1)}, f32[1,16]{1,0:T(1,128)S(1)}) custom-call(f32[4,16,32,128]{3,2,1,0:T(8,128)} %flow.1, s32[16,32,128]{2,1,0:T(8,128)} %regions.1, bf16[32,128,128]{2,1,0:T(8,128)(2,1)} %bitcast.9, bf16[3,32,128]{2,1,0:T(8,128)(2,1)} %bitcast.10, s32[32]{0:T(128)} %bitcast.12, ...), custom_call_target="tpu_custom_call" | custom-call | tf_op jit(solution)/shard_map/pallas_call | solution.py:561
  32.0 1.2 %shard_map.86 = (f32[3,16,32,128]{3,2,1,0:T(8,128)}, f32[3,16,32,128]{3,2,1,0:T(8,128)}, f32[1,16]{1,0:T(1,128)}) custom-call(f32[3,16,32,128]{3,2,1,0:T(8,128)S(1)} %get-tuple-element.9.vn, f32[3,16,32,128]{3,2,1,0:T(8,128)S(1)} %get-tuple-element.10.adj, f32[1,16]{1,0:T(1,128)S(1)} %get-tuple-element.11.sens), custom_call_target="tpu_custom_call" | custom-call | tf_op jit(solution)/shard_map/pallas_call | solution.py:636

commit v7 on v6

--- a/solution.py
+++ b/solution.py
@@ -401,7 +401,7 @@
     lax.fori_loop(0, CX, build_regions, 0)
     packed_ids = pack_edges(lambda x, k: reg[x, 8 * k : 8 * k + 8, :], jnp.zeros((8, TW), jnp.int32))
 
-    onez[...] = by_fine_label(packed_ids)
+    onez[0:TW, :] = by_fine_label(packed_ids)
 
     def store_zmask(pair, rows):
         maskz[pair] = rows
@@ -427,6 +427,8 @@
     wait_walls(2)
     rb2[f] = sb2[f]
 
+    onez[TW : 5 * TW, :] = onelo[0 : 4 * TW, :]
+    onez[5 * TW : 9 * TW, :] = onelo[(CX - 1) * 4 * TW : CX * 4 * TW, :]
     for c in range(3):
         vnp[c] = pack_edges(lambda x, k: vn[c, x, 8 * k : 8 * k + 8, :], jnp.zeros((8, TW), F32))
     receive2()
@@ -452,11 +454,6 @@
     for c in range(3):
         fo[c] = pack_edges(lambda x, k: fp[c, x + 1, TOP + 8 * k : TOP + 8 * k + 8, :], jnp.zeros((8, TW), F32))
     start_z(halo2)
-
-    def plane_sums(x, total):
-        at = pl.ds(pl.multiple_of(x * 4 * TW, TW), 4 * TW)
-        terms = region_terms([total[8 * k : 8 * k + 8] for k in range(4)], lambda k, h: maskhi[x, k, h])
-        return jnp.dot(terms, onelo[at, :], preferred_element_type=F32)
 
     def adjoint_plane(x, carry, last):
         flux_x = []
@@ -488,8 +485,7 @@
     wait_halo(halo2)
     fix2 = [time_step * nup[...] * (packed_halo(fl[c], fh[c]) - fo[c]) for c in range(3)]
     total = fix2[0] * vnp[0] + fix2[1] * vnp[1] + fix2[2] * vnp[2]
-    terms = region_terms([total], lambda k, h: maskz[h])
-    sums = inner[...] + jnp.dot(terms, onez[...], preferred_element_type=F32)
+    edge_terms = [region_terms([total], lambda k, h: maskz[h])]
     for plane, side, face in ((0, 0, 0), (CX - 1, 1, CX)):
         total = None
         for c in range(3):
@@ -498,7 +494,10 @@
             adj[c, plane] = adj[c, plane] + value
             part = value * vn[c, plane]
             total = part if total is None else total + part
-        sums = sums + plane_sums(plane, total)
+        edge_terms.append(
+            region_terms([total[8 * k : 8 * k + 8] for k in range(4)], lambda k, h, x=plane: maskhi[x, k, h]))
+    sums = inner[...] + jnp.dot(
+        jnp.concatenate(edge_terms, axis=1), onez[...], preferred_element_type=F32)
 
     sums = jnp.where(iota((TW // 2, TW), 0) % 8 == iota((TW // 2, TW), 1) % 8, sums, 0.0)
     coarse_rows = [jnp.sum(sums[8 * h : 8 * h + 8], axis=0, keepdims=True) for h in range(8)]
@@ -604,7 +603,7 @@
                 pltpu.VMEM((TW, 3 * TW), BF16),
                 pltpu.VMEM((CX * 4 * TW, TW), BF16),
                 pltpu.VMEM((CX, 4, 4, MSG, TW), BF16),
-                pltpu.VMEM((TW, TW), BF16),
+                pltpu.VMEM((9 * TW, TW), BF16),
                 pltpu.VMEM((4, MSG, TW), BF16),
                 pltpu.VMEM((TW, TW), BF16),
                 pltpu.VMEM((TW // 2, CX * 4 * TW), BF16),

time: 33.5 us -> 33.5 us (level)
  no operation moved by 1% of the time
where the time goes in v7:
time: 33.5 us; the launch traced here: 33.1 us
  Pallas kernels  32.5 us (97%)
  between operations  0.64 us (2%)
    pallas_call x1, Pallas kernels, body(): pl.pallas_call(functools.partial(kernel, nf, nw, tiles), out_shape=(pltpu...  31.3 us
    pallas_call x1, Pallas kernels, body(): pl.pallas_call(write_out, out_shape=tuple((jax.ShapeDtypeStruct(a.shape,...  1.2 us

profile of v7, /device:TPU:8, one launch (start us, length us, event | category | flops | bytes accessed | tf_op | source)
XLA Modules:
  0.0 33.1 jit_solution(11837371101144227310)
XLA Ops:
  0.6 31.3 %shard_map.85 = (f32[3,16,32,128]{3,2,1,0:T(8,128)S(1)}, f32[3,16,32,128]{3,2,1,0:T(8,128)S(1)}, f32[1,16]{1,0:T(1,128)S(1)}) custom-call(f32[4,16,32,128]{3,2,1,0:T(8,128)} %flow.1, s32[16,32,128]{2,1,0:T(8,128)} %regions.1, bf16[32,128,128]{2,1,0:T(8,128)(2,1)} %bitcast.9, bf16[3,32,128]{2,1,0:T(8,128)(2,1)} %bitcast.10, s32[32]{0:T(128)} %bitcast.12, ...), custom_call_target="tpu_custom_call" | custom-call | tf_op jit(solution)/shard_map/pallas_call | solution.py:560
  31.9 1.2 %shard_map.86 = (f32[3,16,32,128]{3,2,1,0:T(8,128)}, f32[3,16,32,128]{3,2,1,0:T(8,128)}, f32[1,16]{1,0:T(1,128)}) custom-call(f32[3,16,32,128]{3,2,1,0:T(8,128)S(1)} %get-tuple-element.9.vn, f32[3,16,32,128]{3,2,1,0:T(8,128)S(1)} %get-tuple-element.10.adj, f32[1,16]{1,0:T(1,128)S(1)} %get-tuple-element.11.sens), custom_call_target="tpu_custom_call" | custom-call | tf_op jit(solution)/shard_map/pallas_call | solution.py:635
